TPU v7x, 512 devices: a whole 4x8x8 slice. The times are simulated.
512 devices in a mesh: shard: 64 (over z, y_lo, core), rep: 8 (over x, y_hi).
Axes of the slice: x: 4, y: 8 (y_hi: 2, y_lo: 4; y = y_hi * 4 + y_lo), z: 8, core: 2. Of those that a mesh axis runs over, the one named last changes fastest.
Arguments:
- entity: float32 [65536, 256], P(('shard', 'rep')), may hold values from -1.5 to 1.5
- rel_weight: float32 [900, 256], replicated, may hold values from -4 to 4
- tile_rel: int32 [16384], P(('shard', 'rep')), may hold values from 0 to 899
- tile_head: int32 [16384], P(('shard', 'rep')), may hold values from 0 to 7
- tile_tail: int32 [16384], P(('shard', 'rep')), may hold values from 0 to 7
- tile_mask: int32 [16384, 128, 128], P(('shard', 'rep')), may hold values 0 or 1
- negatives: int32 [16384, 256], P(('shard', 'rep')), may hold values from 0 to 1023
- tile_count: int32 [512], P(('shard', 'rep')), may hold values from 1 to 32, as said below
Outputs:
- entity_grad: float32 [65536, 256], P(('shard', 'rep'))
- rel_grad: float32 [900, 256], replicated
Inputs may be any that keep to these rules, and one draw needn't show every extreme that they name: `tile_count`: the used slots of a device are its first ones; some device uses all 32.
All inputs are finite; a program needn't handle non-finite values. No bound on the sum of `tile_mask` on one device may be relied on, other than what follows from the above.
Results may differ from a plain program's by a relative error of at most 0.0003.
Values sent between devices are 32-bit elements; how exact they have to be, the bound alone decides.
A program may use at most 64 MiB of HBM per device.

v0:
```python
import jax
import jax.numpy as jnp
from jax import lax
from jax.sharding import PartitionSpec as P


def shifted(block, axis, distance):
    devices = range(lax.axis_size(axis))
    route = [((i - distance) % len(devices), i) for i in devices]
    return lax.ppermute(block, axis, route)


def tile_terms(head, tail, rel_weight, tile_rel, tile_head, tile_tail, tile_mask, negatives, count):
    high = lax.Precision.HIGHEST
    block = tile_mask.shape[1]
    width = head.shape[1]
    blocks = head.shape[0] // block
    head_b = head.reshape(blocks, block, width)
    tail_b = tail.reshape(blocks, block, width)
    group_size = 4
    rounds = (count + group_size - 1) // group_size

    def step(index, carry):
        head_grad, tail_grad, rel_grad = carry
        start = index * group_size
        rels = lax.dynamic_slice_in_dim(tile_rel, start, group_size)
        heads = lax.dynamic_slice_in_dim(tile_head, start, group_size)
        tails = lax.dynamic_slice_in_dim(tile_tail, start, group_size)
        masks = lax.dynamic_slice_in_dim(tile_mask, start, group_size)
        negs = lax.dynamic_slice_in_dim(negatives, start, group_size)
        live = (start + jnp.arange(group_size, dtype=jnp.int32) < count).astype(jnp.float32)
        hrows = head_b[heads]
        trows = tail_b[tails]
        weights = rel_weight[rels]
        nrows = tail[negs]
        scaled = hrows * weights[:, None, :]
        scores = jnp.einsum("tik,tjk->tij", scaled, trows, precision=high)
        grads = -(masks.astype(jnp.float32) * live[:, None, None]) * jax.nn.sigmoid(-scores)
        negsc = jnp.einsum("tik,tjk->tij", scaled, nrows, precision=high)
        ngrads = live[:, None, None] * jax.nn.sigmoid(negsc)
        mixed = jnp.einsum("tij,tjk->tik", grads, trows, precision=high) + jnp.einsum(
            "tij,tjk->tik", ngrads, nrows, precision=high
        )
        dhead = mixed * weights[:, None, :]
        dtail = jnp.einsum("tij,tik->tjk", grads, scaled, precision=high)
        dneg = jnp.einsum("tij,tik->tjk", ngrads, scaled, precision=high)
        dweight = jnp.sum(hrows * mixed, axis=1)
        head_grad = head_grad.reshape(blocks, block, width).at[heads].add(dhead).reshape(-1, width)
        tail_grad = tail_grad.reshape(blocks, block, width).at[tails].add(dtail).reshape(-1, width)
        tail_grad = tail_grad.at[negs.reshape(-1)].add(dneg.reshape(-1, width))
        rel_grad = rel_grad.at[rels].add(dweight)
        return (head_grad, tail_grad, rel_grad)

    start_state = (
        jnp.zeros(head.shape, jnp.float32),
        jnp.zeros(tail.shape, jnp.float32),
        jnp.zeros(rel_weight.shape, jnp.float32),
    )
    return lax.fori_loop(0, rounds, step, start_state)


def local(entity, rel_weight, tile_rel, tile_head, tile_tail, tile_mask, negatives, tile_count):
    head = lax.all_gather(entity, "rep", axis=0, tiled=True)
    tail = shifted(head, "shard", 1)
    head_grad, tail_grad, rel_grad = tile_terms(
        head, tail, rel_weight, tile_rel, tile_head, tile_tail, tile_mask, negatives, tile_count[0]
    )
    returned = shifted(tail_grad, "shard", -1)
    entity_grad = lax.psum_scatter(head_grad + returned, "rep", scatter_dimension=0, tiled=True)
    rel_total = lax.psum(rel_grad, ("shard", "rep"))
    return (entity_grad, rel_total)


def solution(mesh):
    return jax.shard_map(
        local,
        mesh=mesh,
        in_specs=(
            P(("shard", "rep"), None),
            P(),
            P(("shard", "rep")),
            P(("shard", "rep")),
            P(("shard", "rep")),
            P(("shard", "rep"), None, None),
            P(("shard", "rep"), None),
            P(("shard", "rep")),
        ),
        out_specs=(P(("shard", "rep"), None), P()),
        check_vma=False,
    )
```

profile of v0, /device:TPU:1, one launch (start us, length us, event | category | flops | bytes accessed | tf_op | source)
XLA Modules:
  0.0 733.6 jit_solution(3684444154924578298)
XLA Ops:
  8.0 72.7 %all-gather.2.cloned.1.call-done = f32[1024,256]{1,0:T(8,128)} async-done(((f32[128,256]{1,0:T(8,128)}), f32[1024,256]{1,0:T(8,128)}) %all-gather.2.cloned.1.call-update) | async-done | bytes 1048592 | tf_op jit(solution)/shard_map/all_gather | solution.py:63
  80.6 5.9 collective-permute-start
  87.2 11.4 %collective-permute-done = f32[1024,256]{1,0:T(8,128)S(1)} collective-permute-done((f32[1024,256]{1,0:T(8,128)}, f32[1024,256]{1,0:T(8,128)S(1)}, u32[]{:S(2)}, u32[]{:S(2)}) %collective-permute-start) | collective-permute-done | bytes 1048608 | tf_op jit(solution)/shard_map/ppermute | solution.py:10
  100.8 97.8 %while.14 = (s32[]{:T(128)}, f32[1024,256]{1,0:T(8,128)}, f32[1024,256]{1,0:T(8,128)S(1)}, f32[900,256]{1,0:T(8,128)}, s32[]{:T(128)}, /*index=5*/s32[32]{0:T(12...) while((s32[]{:T(128)}, f32[1024,256]{1,0:T(8,128)}, ...), condition=%wide.region_6.7_spmd, body=%wide.region_0.6_spmd.sunk | while | flops 1814439936 | bytes 28422732 | solution.py:59
  104.1 1.8 gather_fusion
  111.1 4.7 gather_fusion.3
  115.7 2.6 fusion.58
  119.1 2.0 fusion.60
  121.2 6.9 scatter_fusion.2
  128.1 2.6 scatter_fusion
  130.7 2.7 scatter_fusion.3
  134.2 1.7 gather_fusion.1
  136.7 1.8 gather_fusion
  143.7 4.7 gather_fusion.3
  148.3 2.6 fusion.58
  151.7 2.0 fusion.60
  153.8 6.9 scatter_fusion.2
  160.7 2.6 scatter_fusion
  163.3 2.7 scatter_fusion.3
  169.3 1.8 gather_fusion
  176.3 4.7 gather_fusion.3
  181.0 2.6 fusion.58
  184.4 2.0 fusion.60
  186.4 6.9 scatter_fusion.2
  193.3 2.6 scatter_fusion
  195.9 2.7 scatter_fusion.3
  198.6 137.0 %collective-permute-start.1 = (f32[1024,256]{1,0:T(8,128)S(1)}, f32[1024,256]{1,0:T(8,128)S(1)}, u32[]{:S(2)}, u32[]{:S(2)}) collective-permute-start(f32[1024,256]{1,0:T(8,128)S(1)} %get-tuple-element.83), channel_id=1, source_target_pairs={{8,0},{16,8},{24,16},{32,24},{40,32},{48,40},{56,48},{64,56},{72,6... | collective-permute-start | bytes 3145736 | tf_op jit(solution)/shard_map/ppermute | solution.py:10
  335.7 2.2 collective-permute-done.1
  337.9 2.3 add.74
  340.3 293.2 %all-reduce.2.cloned.1.call-done = f32[900,256]{1,0:T(8,128)} async-done(((f32[900,256]{1,0:T(8,128)}), f32[900,256]{1,0:T(8,128)}) %all-reduce.2.cloned.1.call-update) | async-done | bytes 921616 | tf_op jit(solution)/shard_map/psum | solution.py:70
  633.5 91.3 %reduce-scatter.2.cloned.1.call-done = f32[128,256]{1,0:T(8,128)} async-done(((f32[1024,256]{1,0:T(8,128)}), f32[128,256]{1,0:T(8,128)}) %reduce-scatter.2.cloned.1.call-update) | async-done | bytes 131088 | tf_op jit(solution)/shard_map/reduce_scatter | solution.py:69
  724.9 2.2 copy.38
  (80 shorter events, 28.9 us)
Async XLA Ops:
  7.2 93.6 %copy-start.3 = (s32[32]{0:T(128)S(1)}, s32[32]{0:T(128)}, u32[]{:S(2)}) copy-start(s32[32]{0:T(128)} %param.14) | copy-start | bytes 388
  7.2 93.6 %copy-start.4 = (s32[32]{0:T(128)S(1)}, s32[32]{0:T(128)}, u32[]{:S(2)}) copy-start(s32[32]{0:T(128)} %param.13) | copy-start | bytes 388
  7.2 93.6 %copy-start.2 = (s32[32]{0:T(128)S(1)}, s32[32]{0:T(128)}, u32[]{:S(2)}) copy-start(s32[32]{0:T(128)} %param.12) | copy-start | bytes 388
  7.2 73.4 %all-gather.2.cloned.1.call-start = ((), (), s32[]{:S(2)}) async-start(), calls=%async_computation.1 | async-start | bytes 1179648 | tf_op jit(solution)/shard_map/all_gather | solution.py:63
  7.9 625.6 %all-reduce.2.cloned.1.call-start = ((), (), s32[]{:S(2)}) async-start(), calls=%async_computation.3 | async-start | bytes 1851392 | tf_op jit(solution)/shard_map/psum | solution.py:70
  80.6 18.0 %collective-permute-start = (f32[1024,256]{1,0:T(8,128)}, f32[1024,256]{1,0:T(8,128)S(1)}, u32[]{:S(2)}, u32[]{:S(2)}) collective-permute-start(f32[1024,256]{1,0:T(8,128)} %all-gather.2.cloned.1.call-done), channel_id=1, source_target_pairs={{504,0},{0,8},{8,16},{16,24},{24,32},{32,40},{40,48},{48,56},{56,6... | collective-permute-start | bytes 3145736 | tf_op jit(solution)/shard_map/ppermute | solution.py:10
  115.7 2.6 copy-start
  115.7 2.6 copy-start.1
  148.3 2.6 copy-start
  148.3 2.6 copy-start.1
  181.0 2.6 copy-start
  181.0 2.6 copy-start.1
  198.6 139.3 %collective-permute-start.1 = (f32[1024,256]{1,0:T(8,128)S(1)}, f32[1024,256]{1,0:T(8,128)S(1)}, u32[]{:S(2)}, u32[]{:S(2)}) collective-permute-start(f32[1024,256]{1,0:T(8,128)S(1)} %get-tuple-element.83), channel_id=1, source_target_pairs={{8,0},{16,8},{24,16},{32,24},{40,32},{48,40},{56,48},{64,56},{72,6... | collective-permute-start | bytes 3145736 | tf_op jit(solution)/shard_map/ppermute | solution.py:10
  335.7 389.2 %reduce-scatter.2.cloned.1.call-start = ((), (), s32[]{:S(2)}) async-start(), calls=%async_computation.2 | async-start | bytes 1179648 | tf_op jit(solution)/shard_map/reduce_scatter | solution.py:69
Sparse Core Ops, SparseCore 0:
  11.2 69.3 all-gather.1
  335.8 297.6 all-reduce.1
  638.6 86.1 reduce-scatter.1
where the time goes:
time: 736 us; the launch traced here: 734 us
  waiting for transfers between devices  471 us (64%)
  starting transfers between devices  143 us (19%)
  other arithmetic  46.3 us (6%)
  local copies, waits for them, and re-layouts  30.8 us (4%)
  matrix products  27 us (4%)
  between operations  14.5 us (2%)
    psum x1, waiting for transfers between devices, local(): rel_total = lax.psum(rel_grad, ('shard', 'rep'))  293 us
    ppermute x2, starting transfers between devices, shifted(): return lax.ppermute(block, axis, route)  143 us
    reduce_scatter x1, waiting for transfers between devices, local(): lax.psum_scatter(head_grad + returned, 'rep', scatter_dimension=0, tiled=...  91.3 us
    all_gather x1, waiting for transfers between devices, local(): head = lax.all_gather(entity, 'rep', axis=0, tiled=True)  72.7 us
    scatter-add x3, other arithmetic, step(): tail_grad = tail_grad.at[negs.reshape(-1)].add(dneg.reshape(-1, width))  20.8 us
  transfers between devices with their start and end apart: 5, of which 5 were waited for; matrix products, arithmetic and copies ran while one was open for 0% of the time, Pallas kernels for 0%

commit v1 on v0

v1 whole, which is shorter than its diff:
```python
import functools

import jax
import jax.numpy as jnp
from jax import lax
from jax.experimental import pallas as pl
from jax.experimental.pallas import tpu as pltpu
from jax.sharding import PartitionSpec as P

MESH = pl.DeviceIdType.MESH
VMEM = pltpu.VMEM
F32 = jnp.float32
BF16 = jnp.bfloat16
BLOCK = 128
WIDTH = 256
BLOCKS = 8
GROUP = 4
REL_PAD = 1024


def place():
    shard = lax.axis_index("shard")
    rep = lax.axis_index("rep")
    core = shard % 2
    y_lo = (shard // 2) % 4
    z = shard // 8
    x = rep // 2
    y = (rep % 2) * 4 + y_lo
    return x, y, z, core


def device(x, y, z, core):
    x = (x + 8) % 4
    y = (y + 16) % 8
    z = (z + 16) % 8
    return ((z * 4 + y % 4) * 2 + core, x * 2 + y // 4)


def chain(y, z, core, far):
    y_lo = y % 4
    step = 2 * core - 1
    z_step = core * (y_lo // 3) - (1 - core) * ((3 - y_lo) // 3)
    return y + step * (5 if far else 1), z + z_step


def greet(partners):
    barrier = pltpu.get_barrier_semaphore()
    for partner in partners:
        pl.semaphore_signal(barrier, inc=1, device_id=partner, device_id_type=MESH)
    pl.semaphore_wait(barrier, len(partners))


def remote(src, dst, send, recv, target):
    return pltpu.make_async_remote_copy(
        src_ref=src, dst_ref=dst, send_sem=send, recv_sem=recv, device_id=target, device_id_type=MESH
    )


def gather_kernel(own_ref, head, tail, ys, yr, xs, xr, cs, cr, ls):
    x, y, z, core = place()
    q = y // 4
    y_lo = y % 4
    left = device(x - 1, y, z, core)
    right = device(x + 1, y, z, core)
    pair = device(x, y + 4, z, core)
    other = device(x, y, z, 1 - core)
    near = chain(y, z, core, False)
    far = chain(y, z, core, True)
    near_dev = device(x, near[0], near[1], 1 - core)
    far_dev = device(x, far[0], far[1], 1 - core)
    greet([left, right, pair, other, near_dev, far_dev])
    mine = 2 * x + q

    q_near = (q + (3 - y_lo) // 3) % 2
    slots = [(head, q), (head, 1 - q), (tail, q_near), (tail, 1 - q_near)]

    def y_copy(k, target, array):
        return remote(own_ref, array.at[mine], ys.at[k], yr.at[k], target)

    def spread(i, from_own=False):
        array, part = slots[i]
        block = 2 * x + part
        src = own_ref if from_own else array.at[block]
        a = remote(src, array.at[block], xs.at[i, 0], xr.at[i, 0], right)
        b = remote(src, array.at[block], xs.at[i, 1], xr.at[i, 1], left)
        return a, b

    def relay(i):
        array, part = slots[i]
        from_left = 2 * ((x + 3) % 4) + part
        from_right = 2 * ((x + 1) % 4) + part
        half = BLOCK // 2
        top = array.at[from_left, pl.ds(0, half)]
        low = array.at[from_right, pl.ds(half, half)]
        return (
            remote(top, top, xs.at[i, 2], xr.at[i, 2], right),
            remote(low, low, xs.at[i, 3], xr.at[i, 3], left),
        )

    def arrived(i):
        array, part = slots[i]
        from_left = 2 * ((x + 3) % 4) + part
        from_right = 2 * ((x + 1) % 4) + part
        opposite = 2 * ((x + 2) % 4) + part
        half = BLOCK // 2
        l = array.at[from_left]
        r = array.at[from_right]
        t = array.at[opposite, pl.ds(0, half)]
        b = array.at[opposite, pl.ds(half, half)]
        return (
            remote(l, l, xs.at[i, 0], xr.at[i, 0], left),
            remote(r, r, xs.at[i, 1], xr.at[i, 1], right),
            remote(t, t, xs.at[i, 2], xr.at[i, 2], left),
            remote(b, b, xs.at[i, 3], xr.at[i, 3], right),
        )

    def across(block, k, own=False):
        src = own_ref if own else head.at[block]
        return remote(src, tail.at[block], cs.at[k], cr.at[k], other)

    is_head = core == 0
    is_next = core == 1

    @pl.when(is_next)
    def _():
        y_copy(1, near_dev, tail).start()

    y_copy(0, pair, head).start()

    @pl.when(is_next)
    def _():
        y_copy(2, far_dev, tail).start()

    for c in spread(0, True):
        c.start()

    @pl.when(is_head)
    def _():
        across(mine, 0, True).start()

    keep = pltpu.make_async_copy(own_ref, head.at[mine], ls)
    keep.start()

    def pass_on(i, k):
        a, b, _, _ = arrived(i)
        ra, rb = relay(i)
        part = slots[i][1]
        a.wait_recv()
        ra.start()
        if k is not None:
            @pl.when(is_head)
            def _():
                across(2 * ((x + 3) % 4) + part, k).start()
        b.wait_recv()
        rb.start()
        if k is not None:
            @pl.when(is_head)
            def _():
                across(2 * ((x + 1) % 4) + part, k + 1).start()

    def y_arrival(k, array, block):
        return remote(array.at[block], array.at[block], ys.at[k], yr.at[k], pair)

    @pl.when(is_head)
    def _():
        y_arrival(1, tail, 2 * x + q_near).wait_recv()
        for c in spread(2):
            c.start()

    pass_on(0, 1)

    y_arrival(0, head, 2 * x + 1 - q).wait_recv()
    for c in spread(1):
        c.start()

    @pl.when(is_head)
    def _():
        across(2 * x + 1 - q, 3).start()
        pass_on(2, None)
        y_arrival(2, tail, 2 * x + 1 - q_near).wait_recv()
        for c in spread(3):
            c.start()

    pass_on(1, 4)

    def finish(i, k):
        _, _, t, b = arrived(i)
        t.wait_recv()
        b.wait_recv()
        if k is not None:
            @pl.when(is_head)
            def _():
                across(2 * ((x + 2) % 4) + slots[i][1], k).start()

    finish(0, 6)
    finish(1, 7)

    @pl.when(is_head)
    def _():
        pass_on(3, None)
        finish(2, None)
        finish(3, None)

    @pl.when(is_next)
    def _():
        partner_blocks = [
            2 * x + q,
            2 * ((x + 3) % 4) + q,
            2 * ((x + 1) % 4) + q,
            2 * x + 1 - q,
            2 * ((x + 3) % 4) + 1 - q,
            2 * ((x + 1) % 4) + 1 - q,
            2 * ((x + 2) % 4) + q,
            2 * ((x + 2) % 4) + 1 - q,
        ]
        for k, block in enumerate(partner_blocks):
            remote(tail.at[block], tail.at[block], cs.at[k], cr.at[k], other).wait_recv()

    keep.wait()
    y_copy(0, pair, head).wait_send()

    @pl.when(is_next)
    def _():
        y_copy(1, near_dev, tail).wait_send()
        y_copy(2, far_dev, tail).wait_send()

    def sent(i):
        for c in spread(i, i == 0):
            c.wait_send()
        for c in relay(i):
            c.wait_send()

    sent(0)
    sent(1)

    @pl.when(is_head)
    def _():
        sent(2)
        sent(3)
        for k in range(8):
            across(mine, k).wait_send()


def gather(entity):
    out = jax.ShapeDtypeStruct((BLOCKS, BLOCK, WIDTH), F32)
    return pl.pallas_call(
        gather_kernel,
        name="gather_partitions",
        out_shape=(out, out),
        in_specs=[pl.BlockSpec(memory_space=VMEM)],
        out_specs=(pl.BlockSpec(memory_space=VMEM), pl.BlockSpec(memory_space=VMEM)),
        scratch_shapes=[
            pltpu.SemaphoreType.DMA((3,)),
            pltpu.SemaphoreType.DMA((3,)),
            pltpu.SemaphoreType.DMA((4, 4)),
            pltpu.SemaphoreType.DMA((4, 4)),
            pltpu.SemaphoreType.DMA((8,)),
            pltpu.SemaphoreType.DMA((8,)),
            pltpu.SemaphoreType.DMA,
        ],
        compiler_params=pltpu.CompilerParams(collective_id=0, has_side_effects=True, vmem_limit_bytes=32 << 20),
    )(entity)


def halves(value):
    hi = value.astype(BF16)
    lo = (value - hi.astype(F32)).astype(BF16)
    return hi, lo


def dot_nt(a, b):
    return lax.dot_general(a, b, (((1,), (1,)), ((), ())), preferred_element_type=F32)


def terms_kernel(
    rel_s, head_s, tail_s, count_s, head, tail, relw, negs, mask, hgrad, tgrad, rgrad,
    t_cols, t_rows, xx, xt, scores, g_hi, g_lo, mixed, tg_t, counts,
):
    group = pl.program_id(0)
    count = count_s[0]
    parts = 4
    rows = GROUP * BLOCK
    step = WIDTH

    @pl.when(group == 0)
    def _():
        hgrad[...] = jnp.zeros_like(hgrad)
        rgrad[...] = jnp.zeros_like(rgrad)
        tg_t[...] = jnp.zeros_like(tg_t)
        for b in range(BLOCKS):
            hi, lo = halves(tail[b])
            at = pl.ds(b * BLOCK, BLOCK)
            t_cols[at, 0:256] = hi
            t_cols[at, 256:512] = hi
            t_cols[at, 512:768] = lo
            n, sub = b // 2, (b % 2) * BLOCK
            t_rows[n, pl.ds(sub, BLOCK), :] = hi
            t_rows[n, pl.ds(256 + sub, BLOCK), :] = hi
            t_rows[n, pl.ds(512 + sub, BLOCK), :] = lo

    @pl.when(group * GROUP < count)
    def _():
        for j in range(GROUP):
            tile = group * GROUP + j
            at = pl.ds(j * BLOCK, BLOCK)
            scaled = head[head_s[tile]] * relw[pl.ds(rel_s[tile], 1), :]
            hi, lo = halves(scaled)
            xx[at, 0:256] = hi
            xx[at, 256:512] = lo
            xx[at, 512:768] = hi
            hi_t, lo_t = halves(scaled.T)
            xt[:, pl.ds(j * BLOCK, BLOCK)] = hi_t
            xt[:, pl.ds(rows + j * BLOCK, BLOCK)] = lo_t
            xt[:, pl.ds(2 * rows + j * BLOCK, BLOCK)] = hi_t
            live = (tile < count).astype(F32)
            drawn = negs[pl.ds(tile, 1), :]
            upper = (lax.broadcasted_iota(jnp.int32, (BLOCKS, 256), 0) == drawn // BLOCK).astype(F32)
            lower = (lax.broadcasted_iota(jnp.int32, (BLOCK, 256), 0) == drawn % BLOCK).astype(F32)
            counts[j] = dot_nt(upper.astype(BF16), lower.astype(BF16)) * live

        def make_scores(n):
            scores[n] = dot_nt(xx[...], t_cols[pl.ds(n * step, step), :])

        def make_grads(n):
            for j in range(GROUP):
                tile = group * GROUP + j
                alive = tile < count
                at = pl.ds(j * BLOCK, BLOCK)
                marked = mask[j].astype(F32)
                for h in range(2):
                    b = 2 * n + h
                    s = scores[n, at, h * BLOCK:(h + 1) * BLOCK]
                    e = jnp.exp(-jnp.abs(s))
                    big = 1.0 / (1.0 + e)
                    small = e * big
                    up = s >= 0.0
                    here = jnp.where(jnp.logical_and(alive, tail_s[tile] == b), 1.0, 0.0).astype(F32)
                    g = counts[j, b:b + 1, :] * jnp.where(up, big, small) - (marked * here) * jnp.where(up, small, big)
                    hi, lo = halves(g)
                    g_hi[n, at, h * BLOCK:(h + 1) * BLOCK] = hi
                    g_lo[n, at, h * BLOCK:(h + 1) * BLOCK] = lo

        def make_tail(n):
            weights = jnp.concatenate([g_hi[n], g_hi[n], g_lo[n]], axis=0)
            tg_t[:, pl.ds(n * step, step)] += jnp.dot(xt[...], weights, preferred_element_type=F32)

        def make_mixed(n):
            rows_in = jnp.concatenate([g_hi[n], g_lo[n], g_hi[n]], axis=1)
            part = jnp.dot(rows_in, t_rows[n], preferred_element_type=F32)
            if n == 0:
                mixed[...] = part
            else:
                mixed[...] += part

        make_scores(0)
        for n in range(parts):
            if n + 1 < parts:
                make_scores(n + 1)
            make_grads(n)
            make_mixed(n)
            make_tail(n)

        for j in range(GROUP):
            tile = group * GROUP + j
            at = pl.ds(j * BLOCK, BLOCK)
            h, r = head_s[tile], rel_s[tile]
            m = mixed[at, :]
            hgrad[h] += m * relw[pl.ds(r, 1), :]
            row = jnp.sum(head[h] * m, axis=0, keepdims=True)
            rgrad[0, pl.ds(r, 1), :] += row[:, 0:128]
            rgrad[1, pl.ds(r, 1), :] += row[:, 128:256]

    @pl.when(group == pl.num_programs(0) - 1)
    def _():
        for b in range(BLOCKS):
            tgrad[b] = tg_t[:, pl.ds(b * BLOCK, BLOCK)].T


def terms(head, tail, rel_weight, tile_rel, tile_head, tile_tail, tile_mask, negatives, count):
    tiles = tile_mask.shape[0]
    groups = tiles // GROUP
    rows = GROUP * BLOCK
    whole = pl.BlockSpec(memory_space=VMEM)

    def mask_at(g, rel_s, head_s, tail_s, count_s):
        return (jnp.minimum(g, (count_s[0] - 1) // GROUP), 0, 0)

    def fixed(n):
        return lambda g, *_: (0,) * n

    part = jax.ShapeDtypeStruct((BLOCKS, BLOCK, WIDTH), F32)
    return pl.pallas_call(
        terms_kernel,
        name="tile_terms",
        out_shape=(part, part, jax.ShapeDtypeStruct((2, REL_PAD, 128), F32)),
        grid_spec=pltpu.PrefetchScalarGridSpec(
            num_scalar_prefetch=4,
            grid=(groups,),
            in_specs=[
                whole,
                whole,
                whole,
                whole,
                pl.BlockSpec((GROUP, BLOCK, BLOCK), mask_at),
            ],
            out_specs=(whole, whole, whole),
            scratch_shapes=[
                VMEM((BLOCKS * BLOCK, 3 * WIDTH), BF16),
                VMEM((4, 3 * WIDTH, WIDTH), BF16),
                VMEM((rows, 3 * WIDTH), BF16),
                VMEM((WIDTH, 3 * rows), BF16),
                VMEM((4, rows, WIDTH), F32),
                VMEM((4, rows, WIDTH), BF16),
                VMEM((4, rows, WIDTH), BF16),
                VMEM((rows, WIDTH), F32),
                VMEM((WIDTH, BLOCKS * BLOCK), F32),
                VMEM((GROUP, BLOCKS, BLOCK), F32),
            ],
        ),
        compiler_params=pltpu.CompilerParams(dimension_semantics=("arbitrary",), vmem_limit_bytes=48 << 20),
    )(tile_rel, tile_head, tile_tail, count, head, tail, rel_weight, negatives, tile_mask)


def reduce_kernel(
    hg, tg, rg, ent, rel,
    t1, part, opp, fwd, out, fin, ysend, yrecv, rc, r1, rx, r2, ry, r3, rz, full, peer,
    cs, cr, ts, tr, fs, fr, os, orr, ys, yr, rcs, rcr, rxs, rxr, rys, ryr, rzs, rzr, ays, ayr, axs, axr, acs, acr,
):
    x, y, z, core = place()
    q = y // 4
    y_lo = y % 4
    left = device(x - 1, y, z, core)
    right = device(x + 1, y, z, core)
    pair = device(x, y + 4, z, core)
    other = device(x, y, z, 1 - core)
    near = chain(y, z, core, False)
    far = chain(y, z, core, True)
    near_dev = device(x, near[0], near[1], 1 - core)
    far_dev = device(x, far[0], far[1], 1 - core)
    x_peers = [device(x + k, y, z, core) for k in range(1, 4)]
    y_peers = [device(x, y + k, z, core) for k in range(1, 8)]
    z_peers = [device(x, y, z + k, core) for k in range(1, 8)]
    greet(x_peers + y_peers + z_peers + [other, near_dev, far_dev])
    is_head = core == 0
    is_next = core == 1
    half = BLOCK // 2
    q_near = (q + (3 - y_lo) // 3) % 2
    slots = [(part, q), (part, 1 - q), (tg, q_near), (tg, 1 - q_near)]
    x_l, x_r, x_o = (x + 3) % 4, (x + 1) % 4, (x + 2) % 4

    rel_core = remote(rg.at[1 - core], rc, rcs, rcr, other)
    rel_core.start()

    to_other = remote(tg, t1, cs, cr, other)

    @pl.when(is_next)
    def _():
        to_other.start()
        part[...] = hg[...]

    def opposite(i):
        array, p = slots[i]
        block = 2 * x_o + p
        return (
            remote(array.at[block, pl.ds(0, half)], fwd.at[i, 0], fs.at[i, 0], fr.at[i, 0], right),
            remote(array.at[block, pl.ds(half, half)], fwd.at[i, 1], fs.at[i, 1], fr.at[i, 1], left),
        )

    def onward(i):
        return (
            remote(out.at[i, 0], fin.at[i, 0], os.at[i, 0], orr.at[i, 0], right),
            remote(out.at[i, 1], fin.at[i, 1], os.at[i, 1], orr.at[i, 1], left),
        )

    def start_opposite(i):
        for c in opposite(i):
            c.start()

    def add_and_send(i):
        array, p = slots[i]
        a, b = opposite(i)
        to_right, to_left = onward(i)
        a.wait_recv()
        out[i, 0, 0:half, :] = array[2 * x_r + p, 0:half, :] + fwd[i, 0]
        out[i, 0, half:BLOCK, :] = array[2 * x_r + p, half:BLOCK, :]
        to_right.start()
        b.wait_recv()
        out[i, 1, half:BLOCK, :] = array[2 * x_l + p, half:BLOCK, :] + fwd[i, 1]
        out[i, 1, 0:half, :] = array[2 * x_l + p, 0:half, :]
        to_left.start()

    def total(i):
        array, p = slots[i]
        to_right, to_left = onward(i)
        to_right.wait_recv()
        to_left.wait_recv()
        return array[2 * x + p] + fin[i, 0] + fin[i, 1]

    @pl.when(is_head)
    def _():
        start_opposite(2)
        start_opposite(3)

    @pl.when(is_next)
    def _():
        start_opposite(0)
        start_opposite(1)

    rel_core.wait_recv()
    r1[...] = rg[core] + rc[...]

    def rel_x(k):
        to = (x + k) % 4
        return remote(r1.at[pl.ds(pl.multiple_of(to * 256, 256), 256)], rx.at[k - 1], rxs.at[k - 1], rxr.at[k - 1], x_peers[k - 1])

    for k in range(1, 4):
        rel_x(k).start()

    @pl.when(is_head)
    def _():
        to_other.wait_recv()
        part[...] = hg[...] + t1[...]
        start_opposite(0)
        start_opposite(1)
        add_and_send(2)
        add_and_send(3)

    add_and_send(1)
    add_and_send(0)

    for k in range(1, 4):
        rel_x(k).wait_recv()
    r2[...] = r1[pl.ds(pl.multiple_of(x * 256, 256), 256), :] + rx[0] + rx[1] + rx[2]

    def rel_y(k):
        to = (y + k) % 8
        return remote(r2.at[pl.ds(pl.multiple_of(to * 32, 32), 32)], ry.at[k - 1], rys.at[k - 1], ryr.at[k - 1], y_peers[k - 1])

    for k in range(1, 8):
        rel_y(k).start()

    def along_y(k, target):
        return remote(ysend.at[k], yrecv.at[k], ys.at[k], yr.at[k], target)

    @pl.when(is_head)
    def _():
        ysend[1] = total(2)
        along_y(1, near_dev).start()
        ysend[2] = total(3)
        along_y(2, far_dev).start()

    ysend[0] = total(1)
    along_y(0, pair).start()

    for k in range(1, 8):
        rel_y(k).wait_recv()
    acc = r2[pl.ds(pl.multiple_of(y * 32, 32), 32), :]
    for k in range(7):
        acc = acc + ry[k]
    rz[0] = acc
    r3[...] = acc

    def rel_z(k):
        return remote(r3, rz.at[k], rzs.at[k - 1], rzr.at[k - 1], z_peers[k - 1])

    for k in range(1, 8):
        rel_z(k).start()

    ent[...] = total(0)

    for k in range(1, 8):
        rel_z(k).wait_recv()
    acc = rz[z]
    acc = rz[(z + 8) % 8]
    for i in range(1, 8):
        acc = acc + rz[(z - i + 8) % 8]
    chunk = pl.ds(pl.multiple_of(x * 256 + y * 32, 32), 32)
    full[chunk, :] = acc

    def gather_y(k):
        return remote(full.at[chunk], full.at[chunk], ays.at[k - 1], ayr.at[k - 1], y_peers[k - 1])

    def gather_y_in(k):
        src = pl.ds(pl.multiple_of(x * 256 + ((y - k + 8) % 8) * 32, 32), 32)
        return remote(full.at[src], full.at[src], ays.at[k - 1], ayr.at[k - 1], y_peers[k - 1])

    for k in range(1, 8):
        gather_y(k).start()
    for k in range(1, 8):
        gather_y_in(k).wait_recv()

    slab = pl.ds(pl.multiple_of(x * 256, 256), 256)

    def gather_x(k):
        return remote(full.at[slab], full.at[slab], axs.at[k - 1], axr.at[k - 1], x_peers[k - 1])

    def gather_x_in(k):
        src = pl.ds(pl.multiple_of(((x - k + 4) % 4) * 256, 256), 256)
        return remote(full.at[src], full.at[src], axs.at[k - 1], axr.at[k - 1], x_peers[k - 1])

    for k in range(1, 4):
        gather_x(k).start()

    along_y(0, pair).wait_recv()
    ent[...] += yrecv[0]

    @pl.when(is_next)
    def _():
        along_y(1, near_dev).wait_recv()
        along_y(2, far_dev).wait_recv()
        ent[...] += yrecv[1] + yrecv[2]

    for k in range(1, 4):
        gather_x_in(k).wait_recv()

    swap = remote(full, peer, acs, acr, other)
    swap.start()
    n = rel.shape[0]

    @pl.when(is_head)
    def _():
        rel[:, 0:128] = full[0:n, :]

    @pl.when(is_next)
    def _():
        rel[:, 128:256] = full[0:n, :]

    swap.wait_recv()

    @pl.when(is_head)
    def _():
        rel[:, 128:256] = peer[0:n, :]

    @pl.when(is_next)
    def _():
        rel[:, 0:128] = peer[0:n, :]

    swap.wait_send()
    rel_core.wait_send()
    for k in range(1, 4):
        rel_x(k).wait_send()
        gather_x(k).wait_send()
    for k in range(1, 8):
        rel_y(k).wait_send()
        rel_z(k).wait_send()
        gather_y(k).wait_send()

    def sent(i):
        for c in opposite(i):
            c.wait_send()
        for c in onward(i):
            c.wait_send()

    sent(0)
    sent(1)
    along_y(0, pair).wait_send()

    @pl.when(is_head)
    def _():
        sent(2)
        sent(3)
        along_y(1, near_dev).wait_send()
        along_y(2, far_dev).wait_send()

    @pl.when(is_next)
    def _():
        to_other.wait_send()


def reduce(hg, tg, rg, relations):
    whole = pl.BlockSpec(memory_space=VMEM)
    dma = pltpu.SemaphoreType.DMA
    return pl.pallas_call(
        reduce_kernel,
        name="reduce_gradients",
        out_shape=(jax.ShapeDtypeStruct((BLOCK, WIDTH), F32), jax.ShapeDtypeStruct((relations, WIDTH), F32)),
        in_specs=[whole] * 3,
        out_specs=(whole, whole),
        scratch_shapes=[
            VMEM((BLOCKS, BLOCK, WIDTH), F32),
            VMEM((BLOCKS, BLOCK, WIDTH), F32),
            VMEM((8, 128), F32),
            VMEM((4, 2, BLOCK // 2, WIDTH), F32),
            VMEM((4, 2, BLOCK, WIDTH), F32),
            VMEM((4, 2, BLOCK, WIDTH), F32),
            VMEM((3, BLOCK, WIDTH), F32),
            VMEM((3, BLOCK, WIDTH), F32),
            VMEM((REL_PAD, 128), F32),
            VMEM((REL_PAD, 128), F32),
            VMEM((3, 256, 128), F32),
            VMEM((256, 128), F32),
            VMEM((7, 32, 128), F32),
            VMEM((32, 128), F32),
            VMEM((8, 32, 128), F32),
            VMEM((REL_PAD, 128), F32),
            VMEM((REL_PAD, 128), F32),
            dma, dma, dma, dma,
            dma((4, 2)), dma((4, 2)), dma((4, 2)), dma((4, 2)),
            dma((3,)), dma((3,)),
            dma, dma,
            dma((3,)), dma((3,)),
            dma((7,)), dma((7,)),
            dma((7,)), dma((7,)),
            dma((7,)), dma((7,)),
            dma((3,)), dma((3,)),
            dma, dma,
        ],
        compiler_params=pltpu.CompilerParams(collective_id=1, has_side_effects=True, vmem_limit_bytes=40 << 20),
    )(hg, tg, rg)


def local(entity, rel_weight, tile_rel, tile_head, tile_tail, tile_mask, negatives, tile_count):
    head, tail = gather(entity)
    hg, tg, rg = terms(head, tail, rel_weight, tile_rel, tile_head, tile_tail, tile_mask, negatives, tile_count)
    return reduce(hg, tg, rg, rel_weight.shape[0])


def solution(mesh):
    return jax.shard_map(
        local,
        mesh=mesh,
        in_specs=(
            P(("shard", "rep"), None),
            P(),
            P(("shard", "rep")),
            P(("shard", "rep")),
            P(("shard", "rep")),
            P(("shard", "rep"), None, None),
            P(("shard", "rep"), None),
            P(("shard", "rep")),
        ),
        out_specs=(P(("shard", "rep"), None), P()),
        check_vma=False,
    )
```

time: 736 us -> 123 us (0.17)
  waiting for transfers between devices: 471 us -> 0 us
  starting transfers between devices: 143 us -> 0 us
  Pallas kernels: 0 us -> 115 us
  other arithmetic: 46.3 us -> 0 us
  matrix products: 27 us -> 0 us
  local copies, waits for them, and re-layouts: 30.8 us -> 6.38 us
  between operations: 14.5 us -> 1.32 us
    psum x1 -> x0, waiting for transfers between devices: 293 us -> none  [local(): rel_total = lax.psum(rel_grad, ('shard', 'rep'))]
    ppermute x2 -> x0, starting transfers between devices: 143 us -> none  [shifted(): return lax.ppermute(block, axis, route)]
    pallas_call x0 -> x3, Pallas kernels: none -> 115 us  [the longest x1 63.3 us: reduce(): pl.pallas_call(reduce_kernel, name='reduce_gradients', out_shape=(jax.Sha...]
    reduce_scatter x1 -> x0, waiting for transfers between devices: 91.3 us -> none  [local(): lax.psum_scatter(head_grad + returned, 'rep', scatter_dimension=0, tiled=...]
    all_gather x1 -> x0, waiting for transfers between devices: 72.7 us -> none  [local(): head = lax.all_gather(entity, 'rep', axis=0, tiled=True)]
    scatter-add x12 -> x0, other arithmetic: 39.3 us -> none  [the longest x3 20.8 us: step(): tail_grad = tail_grad.at[negs.reshape(-1)].add(dneg.reshape(-1, width))]
    dot_general x18 -> x0, matrix products: 27 us -> none  [the longest x3 7.67 us: step(): negsc = jnp.einsum('tik,tjk->tij', scaled, nrows, precision=high)]
    gather x12 -> x0, local copies, waits for them, and re-layouts: 26.4 us -> none  [the longest x3 14 us: step(): nrows = tail[negs]]
  transfers between devices with their start and end apart: 5 -> 0, of which waited for: 5 -> 0; matrix products, arithmetic and copies ran while one was open for 0% -> 0% of each run, Pallas kernels for 0% -> 0%
where the time goes in v1:
time: 123 us; the launch traced here: 122 us
  Pallas kernels  115 us (93%)
  local copies, waits for them, and re-layouts  6.38 us (5%)
  between operations  1.32 us (1%)
    pallas_call x1, Pallas kernels, reduce(): pl.pallas_call(reduce_kernel, name='reduce_gradients', out_shape=(jax.Sha...  63.3 us
    pallas_call x1, Pallas kernels, gather(): pl.pallas_call(gather_kernel, name='gather_partitions', out_shape=(out, o...  34.6 us
    pallas_call x1, Pallas kernels, terms(): pl.pallas_call(terms_kernel, name='tile_terms', out_shape=(part, part, ja...  16.7 us
    unnamed x14, local copies, waits for them, and re-layouts  6.38 us

profile of v1, /device:TPU:1, one launch (start us, length us, event | category | flops | bytes accessed | tf_op | source)
XLA Modules:
  0.0 122.4 jit_solution(1909792595155848076)
XLA Ops:
  1.3 0.0 copy-start.1
  1.3 0.9 copy-done.1
  2.2 34.6 %gather_partitions.1 = (f32[8,128,256]{2,1,0:T(8,128)S(1)}, f32[8,128,256]{2,1,0:T(8,128)S(1)}) custom-call(f32[128,256]{1,0:T(8,128)S(1)} %copy-done.1), custom_call_target="tpu_custom_call" | custom-call | tf_op jit(solution)/shard_map/gather_partitions/pallas_call | solution.py:246
  36.8 0.0 copy-start
  36.8 1.2 copy-done
  38.0 0.0 copy-start.2
  38.0 0.8 copy-done.2
  38.7 0.0 copy-start.3
  38.7 0.7 copy-done.3
  39.4 0.0 copy-start.4
  39.4 0.7 copy-done.4
  40.1 0.0 copy-start.5
  40.1 0.7 copy-done.5
  40.7 16.7 %tile_terms.1 = (f32[8,128,256]{2,1,0:T(8,128)S(1)}, f32[8,128,256]{2,1,0:T(8,128)S(1)}, f32[2,1024,128]{2,1,0:T(8,128)S(1)}) custom-call(s32[32]{0:T(128)S(1)} %copy-done.3, s32[32]{0:T(128)S(1)} %copy-done.4, s32[32]{0:T(128)S(1)} %copy-done.5, s32[1]{0:T(128)S(6)} %copy.12.count_s, f32[8,128,256]{2,1,0:T(8,128)S(1)} %get-tuple-element.7.head, ...), custom_call_target="tpu_custom_call" | custom-call | tf_op jit(solution)/shard_map/tile_terms/pallas_call | solution.py:392
  57.5 63.3 %reduce_gradients.1 = (f32[128,256]{1,0:T(8,128)S(1)}, f32[900,256]{1,0:T(8,128)S(1)}) custom-call(f32[8,128,256]{2,1,0:T(8,128)S(1)} %get-tuple-element.9.hg, f32[8,128,256]{2,1,0:T(8,128)S(1)} %get-tuple-element.10.tg, f32[2,1024,128]{2,1,0:T(8,128)S(1)} %get-tuple-element.11.rg), custom_call_target="tpu_custom_call" | custom-call | tf_op jit(solution)/shard_map/reduce_gradients/pallas_call | solution.py:673
  120.8 0.7 copy.13
  121.5 0.9 copy.14
Async XLA Ops:
  1.3 0.9 copy-start.1
  36.8 1.2 copy-start
  38.0 0.8 copy-start.2
  38.7 0.7 copy-start.3
  39.4 0.7 copy-start.4
  40.1 0.7 copy-start.5

commit v2 on v0

v2 whole, which is shorter than its diff:
```python
import functools

import jax
import jax.numpy as jnp
from jax import lax
from jax.experimental import pallas as pl
from jax.experimental.pallas import tpu as pltpu
from jax.sharding import PartitionSpec as P

MESH = pl.DeviceIdType.MESH
VMEM = pltpu.VMEM
F32 = jnp.float32
BF16 = jnp.bfloat16
BLOCK = 128
WIDTH = 256
BLOCKS = 8
GROUP = 8
REL_PAD = 1024


def place():
    shard = lax.axis_index("shard")
    rep = lax.axis_index("rep")
    core = shard % 2
    y_lo = (shard // 2) % 4
    z = shard // 8
    x = rep // 2
    y = (rep % 2) * 4 + y_lo
    return x, y, z, core


def device(x, y, z, core):
    x = (x + 8) % 4
    y = (y + 16) % 8
    z = (z + 16) % 8
    return ((z * 4 + y % 4) * 2 + core, x * 2 + y // 4)


def greet(partners):
    barrier = pltpu.get_barrier_semaphore()
    for partner in partners:
        pl.semaphore_signal(barrier, inc=1, device_id=partner, device_id_type=MESH)
    pl.semaphore_wait(barrier, len(partners))


def remote(src, dst, send, recv, target):
    return pltpu.make_async_remote_copy(
        src_ref=src, dst_ref=dst, send_sem=send, recv_sem=recv, device_id=target, device_id_type=MESH
    )


def gather_kernel(
    own_ref, relw_in, negs_in, mask_in, rel_in, head_in, tail_in,
    head, tail, relw, negs, mask, rel_s, head_s, tail_s,
    ys, yr, xs, xr, cs, cr, ls, ms,
):
    x, y, z, core = place()
    brought = [(relw_in, relw), (negs_in, negs), (mask_in, mask), (rel_in, rel_s), (head_in, head_s), (tail_in, tail_s)]
    local_copies = [pltpu.make_async_copy(src, dst, ms.at[k]) for k, (src, dst) in enumerate(brought)]
    for c in local_copies:
        c.start()
    q = y // 4
    y_lo = y % 4
    pair = device(x, y + 4, z, core)
    other = device(x, y, z, 1 - core)
    x_peers = [device(x + k, y, z, core) for k in range(1, 4)]
    chain_dev = device(x, y + 2 * core - 1, z + core * (y_lo // 3) - (1 - core) * ((3 - y_lo) // 3), 1 - core)
    is_head = core == 0
    is_next = core == 1
    mine = 2 * x + q
    q_near = (q + (3 - y_lo) // 3) % 2
    half = BLOCK // 2
    keep = pltpu.make_async_copy(own_ref, head.at[mine], ls)
    keep.start()
    greet([pair, other, chain_dev] + x_peers)

    streams = [
        (head, q, 0, BLOCK),
        (tail, q_near, 0, BLOCK),
        (head, 1 - q, 0, half),
        (head, 1 - q, half, half),
        (tail, 1 - q_near, 0, half),
        (tail, 1 - q_near, half, half),
    ]

    def piece(i, xx):
        array, part, first, rows = streams[i]
        return array.at[2 * xx + part, pl.ds(first, rows)]

    def along_x(i, k):
        src = own_ref if i == 0 else piece(i, x)
        return remote(src, piece(i, x), xs.at[i, k - 1], xr.at[i, k - 1], x_peers[k - 1])

    def from_x(i, k):
        at = piece(i, (x - k + 4) % 4)
        return remote(at, at, xs.at[i, k - 1], xr.at[i, k - 1], x_peers[k - 1])

    def spread(i):
        for k in (1, 3, 2):
            along_x(i, k).start()

    def pair_copy(h):
        rows = pl.ds(h * half, half)
        return remote(own_ref.at[rows], head.at[mine, rows], ys.at[h], yr.at[h], pair)

    def pair_in(h):
        at = head.at[2 * x + 1 - q, pl.ds(h * half, half)]
        return remote(at, at, ys.at[h], yr.at[h], pair)

    near_copy = remote(own_ref, tail.at[mine], ys.at[2], yr.at[2], chain_dev)
    near_at = tail.at[2 * x + q_near]
    near_in = remote(near_at, near_at, ys.at[2], yr.at[2], chain_dev)

    def far_copy(h):
        at = (2 * x + 1 - q, pl.ds(h * half, half))
        return remote(head.at[at], tail.at[at], ys.at[3 + h], yr.at[3 + h], chain_dev)

    def far_in(h):
        at = tail.at[2 * x + 1 - q_near, pl.ds(h * half, half)]
        return remote(at, at, ys.at[3 + h], yr.at[3 + h], chain_dev)

    shared = [2 * ((x + k) % 4) + part for part in (q, 1 - q) for k in range(4)]

    def across(n):
        src = own_ref if n == 0 else head.at[shared[n]]
        return remote(src, tail.at[shared[n]], cs.at[n], cr.at[n], other)

    def across_in(n):
        return remote(tail.at[shared[n]], tail.at[shared[n]], cs.at[n], cr.at[n], other)

    @pl.when(is_next)
    def _():
        near_copy.start()

    pair_copy(0).start()
    pair_copy(1).start()
    spread(0)

    @pl.when(is_head)
    def _():
        across(0).start()
        near_in.wait_recv()
        spread(1)

    for h in range(2):
        pair_in(h).wait_recv()

        @pl.when(is_next)
        def _():
            far_copy(h).start()

        spread(2 + h)

    @pl.when(is_head)
    def _():
        across(4).start()
        far_in(0).wait_recv()
        spread(4)
        far_in(1).wait_recv()
        spread(5)

    for k in (3, 1, 2):
        from_x(0, (4 - k) % 4).wait_recv()

        @pl.when(is_head)
        def _():
            across(k).start()

    for k in (3, 1, 2):
        from_x(2, (4 - k) % 4).wait_recv()
        from_x(3, (4 - k) % 4).wait_recv()

        @pl.when(is_head)
        def _():
            across(4 + k).start()

    @pl.when(is_head)
    def _():
        for i in (1, 4, 5):
            for k in range(1, 4):
                from_x(i, k).wait_recv()

    @pl.when(is_next)
    def _():
        for n in range(8):
            across_in(n).wait_recv()

    keep.wait()
    for c in local_copies:
        c.wait()
    for h in range(2):
        pair_copy(h).wait_send()
    for i in (0, 2, 3):
        for k in range(1, 4):
            along_x(i, k).wait_send()

    @pl.when(is_head)
    def _():
        for i in (1, 4, 5):
            for k in range(1, 4):
                along_x(i, k).wait_send()
        for n in range(8):
            across(n).wait_send()

    @pl.when(is_next)
    def _():
        near_copy.wait_send()
        far_copy(0).wait_send()
        far_copy(1).wait_send()


def gather(entity, rel_weight, negatives, tile_mask, tile_rel, tile_head, tile_tail):
    hbm = pl.BlockSpec(memory_space=pltpu.HBM)
    whole = pl.BlockSpec(memory_space=VMEM)
    scalars = pl.BlockSpec(memory_space=pltpu.SMEM)
    part = jax.ShapeDtypeStruct((BLOCKS, BLOCK, WIDTH), F32)
    operands = [entity, rel_weight, negatives, tile_mask, tile_rel, tile_head, tile_tail]
    operands = [pltpu.with_memory_space_constraint(a, pltpu.HBM) for a in operands]
    dma = pltpu.SemaphoreType.DMA
    return pl.pallas_call(
        gather_kernel,
        name="gather_partitions",
        out_shape=(part, part, *[jax.ShapeDtypeStruct(a.shape, a.dtype) for a in operands[1:]]),
        in_specs=[hbm] * 7,
        out_specs=(whole, whole, whole, whole, whole, scalars, scalars, scalars),
        scratch_shapes=[dma((5,)), dma((5,)), dma((6, 3)), dma((6, 3)), dma((8,)), dma((8,)), dma, dma((6,))],
        compiler_params=pltpu.CompilerParams(collective_id=0, has_side_effects=True, vmem_limit_bytes=32 << 20),
    )(*operands)


def halves(value):
    hi = value.astype(BF16)
    lo = (value - hi.astype(F32)).astype(BF16)
    return hi, lo


def dot_nt(a, b):
    return lax.dot_general(a, b, (((1,), (1,)), ((), ())), preferred_element_type=F32)


def terms_kernel(
    rel_s, head_s, tail_s, count_s, head, tail, relw, negs, mask, hgrad, tgrad, listed,
    t_cols, t_rows, xx, xt, scores, g_hi, g_lo, mixed, tg_t, counts,
):
    count = count_s[0]
    parts = 4
    rows = GROUP * BLOCK
    step = WIDTH
    tiles = mask.shape[0]

    hgrad[...] = jnp.zeros_like(hgrad)
    listed[...] = jnp.zeros_like(listed)
    tg_t[...] = jnp.zeros_like(tg_t)
    for b in range(BLOCKS):
        hi, lo = halves(tail[b])
        at = pl.ds(b * BLOCK, BLOCK)
        t_cols[at, 0:256] = hi
        t_cols[at, 256:512] = hi
        t_cols[at, 512:768] = lo
        n, sub = b // 2, (b % 2) * BLOCK
        t_rows[n, pl.ds(sub, BLOCK), :] = hi
        t_rows[n, pl.ds(256 + sub, BLOCK), :] = hi
        t_rows[n, pl.ds(512 + sub, BLOCK), :] = lo

    lane = lax.broadcasted_iota(jnp.int32, (8, 128), 1) % tiles
    ids = jnp.zeros((8, 128), F32)
    for tile in range(tiles):
        ids = jnp.where(lane == tile, rel_s[tile].astype(F32), ids)
    for c in range(2):
        listed[c, tiles:tiles + 8, :] = ids

    def do_group(group, carry):
        for j in range(GROUP):
            tile = group * GROUP + j
            at = pl.ds(j * BLOCK, BLOCK)
            scaled = head[head_s[tile]] * relw[pl.ds(rel_s[tile], 1), :]
            hi, lo = halves(scaled)
            xx[at, 0:256] = hi
            xx[at, 256:512] = lo
            xx[at, 512:768] = hi
            hi_t, lo_t = halves(scaled.T)
            xt[:, pl.ds(j * BLOCK, BLOCK)] = hi_t
            xt[:, pl.ds(rows + j * BLOCK, BLOCK)] = lo_t
            xt[:, pl.ds(2 * rows + j * BLOCK, BLOCK)] = hi_t
            live = (tile < count).astype(F32)
            drawn = negs[pl.ds(tile, 1), :]
            upper = (lax.broadcasted_iota(jnp.int32, (BLOCKS, 256), 0) == drawn // BLOCK).astype(F32)
            lower = (lax.broadcasted_iota(jnp.int32, (BLOCK, 256), 0) == drawn % BLOCK).astype(F32)
            counts[j] = dot_nt(upper.astype(BF16), lower.astype(BF16)) * live

        def make_scores(n):
            scores[n] = dot_nt(xx[...], t_cols[pl.ds(n * step, step), :])

        def make_grads(n):
            for j in range(GROUP):
                tile = group * GROUP + j
                alive = tile < count
                at = pl.ds(j * BLOCK, BLOCK)
                marked = mask[tile].astype(F32)
                for h in range(2):
                    b = 2 * n + h
                    s = scores[n, at, h * BLOCK:(h + 1) * BLOCK]
                    e = jnp.exp(-jnp.abs(s))
                    big = 1.0 / (1.0 + e)
                    small = e * big
                    up = s >= 0.0
                    here = jnp.where(jnp.logical_and(alive, tail_s[tile] == b), 1.0, 0.0).astype(F32)
                    g = counts[j, b:b + 1, :] * jnp.where(up, big, small) - (marked * here) * jnp.where(up, small, big)
                    hi, lo = halves(g)
                    g_hi[n, at, h * BLOCK:(h + 1) * BLOCK] = hi
                    g_lo[n, at, h * BLOCK:(h + 1) * BLOCK] = lo

        def make_tail(n):
            weights = jnp.concatenate([g_hi[n], g_hi[n], g_lo[n]], axis=0)
            tg_t[:, pl.ds(n * step, step)] += jnp.dot(xt[...], weights, preferred_element_type=F32)

        def make_mixed(n):
            rows_in = jnp.concatenate([g_hi[n], g_lo[n], g_hi[n]], axis=1)
            part = jnp.dot(rows_in, t_rows[n], preferred_element_type=F32)
            if n == 0:
                mixed[...] = part
            else:
                mixed[...] += part

        make_scores(0)
        for n in range(parts):
            if n + 1 < parts:
                make_scores(n + 1)
            make_grads(n)
            make_mixed(n)
            make_tail(n)

        for j in range(GROUP):
            tile = group * GROUP + j
            at = pl.ds(j * BLOCK, BLOCK)
            h, r = head_s[tile], rel_s[tile]
            m = mixed[at, :]
            hgrad[h] += m * relw[pl.ds(r, 1), :]
            row = jnp.sum(head[h] * m, axis=0, keepdims=True)
            listed[0, pl.ds(tile, 1), :] = row[:, 0:128]
            listed[1, pl.ds(tile, 1), :] = row[:, 128:256]
        return carry

    lax.fori_loop(0, (count + GROUP - 1) // GROUP, do_group, 0)
    for b in range(BLOCKS):
        tgrad[b] = tg_t[:, pl.ds(b * BLOCK, BLOCK)].T


def terms(head, tail, relw, negs, mask, rel_s, head_s, tail_s, count_s):
    rows = GROUP * BLOCK
    tiles = mask.shape[0]
    whole = pl.BlockSpec(memory_space=VMEM)
    scalars = pl.BlockSpec(memory_space=pltpu.SMEM)
    part = jax.ShapeDtypeStruct((BLOCKS, BLOCK, WIDTH), F32)
    return pl.pallas_call(
        terms_kernel,
        name="tile_terms",
        out_shape=(part, part, jax.ShapeDtypeStruct((2, tiles + 8, 128), F32)),
        in_specs=[scalars] * 4 + [whole] * 5,
        out_specs=(whole, whole, whole),
        scratch_shapes=[
            VMEM((BLOCKS * BLOCK, 3 * WIDTH), BF16),
            VMEM((4, 3 * WIDTH, WIDTH), BF16),
            VMEM((rows, 3 * WIDTH), BF16),
            VMEM((WIDTH, 3 * rows), BF16),
            VMEM((4, rows, WIDTH), F32),
            VMEM((4, rows, WIDTH), BF16),
            VMEM((4, rows, WIDTH), BF16),
            VMEM((rows, WIDTH), F32),
            VMEM((WIDTH, BLOCKS * BLOCK), F32),
            VMEM((GROUP, BLOCKS, BLOCK), F32),
        ],
        compiler_params=pltpu.CompilerParams(vmem_limit_bytes=40 << 20),
    )(rel_s, head_s, tail_s, count_s, head, tail, relw, negs, mask)


def reduce_kernel(
    hg, tg, listed, ent, rel,
    lists, tin, out, fin, ysend, yrecv, p, sy, sz, fy, fz, full, peer,
    ls, lr, ts, tr, xs, xr, ps, pr, rys, ryr, rzs, rzr, bys, byr, bzs, bzr, ays, ayr, azs, azr, gxs, gxr, gcs, gcr,
):
    x, y, z, core = place()
    q = y // 4
    pair = device(x, y + 4, z, core)
    other = device(x, y, z, 1 - core)
    x_peers = [device(x + k, y, z, core) for k in range(1, 4)]
    x_over = [device(x + k, y, z, 1 - core) for k in range(1, 4)]
    y_peers = [device(x, y + k, z, core) for k in range(1, 8)]
    z_peers = [device(x, y, z + k, core) for k in range(1, 8)]
    y_lo = y % 4
    down = device(x, y - 1, z - (3 - y_lo) // 3, 1)
    up = device(x, y + 1, z + y_lo // 3, 0)
    is_head = core == 0
    is_next = core == 1
    chain_dev = device(x, y + 2 * core - 1, z + core * (y_lo // 3) - (1 - core) * ((3 - y_lo) // 3), 1 - core)
    greet(x_peers + x_over + y_peers + z_peers + [other, chain_dev])
    me = core * 4 + x
    tiles = listed.shape[1] - 8

    targets = [(x_peers[k - 1], core, k - 1) for k in range(1, 4)]
    targets += [(x_over[k - 1], 1 - core, 2 + k) for k in range(1, 4)]
    targets += [(other, 1 - core, 6)]

    def list_copy(i):
        target, columns, k = targets[i]
        return remote(listed.at[columns], lists.at[me], ls, lr, target)

    for i in range(7):
        list_copy(i).start()
    lists[me] = listed[core]

    def tail_block(i, q_of):
        parity = 1 - q_of if i < 4 else q_of
        return 2 * ((x + 1 + i % 4) % 4) + parity

    q_down = ((y + 7) % 8) // 4

    def tail_copy(i, q_of, target):
        block = tail_block(i, q_of)
        return remote(tg.at[block], tin.at[i], ts.at[i], tr.at[i], target)

    @pl.when(is_head)
    def _():
        for i in range(8):
            tail_copy(i, q_down, down).start()

    @pl.when(is_next)
    def _():
        for i in range(8):
            tail_copy(i, q, other).start()

    seven = remote(lists.at[pl.ds(0, 7)], lists.at[pl.ds(0, 7)], ls, lr, other)
    seven.wait_recv()
    lane = lax.broadcasted_iota(jnp.int32, (1, 128), 1) // tiles
    picked = []
    for g in range(2):
        row = jnp.zeros((1, 128), F32)
        for d in range(4):
            row = jnp.where(lane == d, lists[g * 4 + d, tiles:tiles + 1, :], row)
        picked.append(row)
    ids = jnp.concatenate(picked, axis=1)
    target_row = (lax.broadcasted_iota(jnp.int32, (256, 256), 0) + x * 256).astype(F32)
    chosen = (target_row == ids).astype(F32).astype(BF16)
    rows = jnp.concatenate([lists[d, 0:tiles, :] for d in range(8)], axis=0)
    hi = rows.astype(BF16)
    rest = rows - hi.astype(F32)
    mid = rest.astype(BF16)
    low = (rest - mid.astype(F32)).astype(BF16)
    placed = jnp.dot(chosen, hi, preferred_element_type=F32)
    placed = placed + jnp.dot(chosen, mid, preferred_element_type=F32)
    placed = placed + jnp.dot(chosen, low, preferred_element_type=F32)
    p[...] = placed

    def chunk(k, base=0):
        return pl.ds(pl.multiple_of(base + k * 16, 16), 16)

    def all_of(buffer, send, recv):
        return remote(buffer, buffer, send, recv, other)

    def first_y(k):
        return remote(p.at[chunk((y + k) % 8)], sy.at[k - 1], rys, ryr, y_peers[k - 1])

    def first_z(k):
        return remote(p.at[chunk((z + k) % 8, 128)], sz.at[k - 1], rzs, rzr, z_peers[k - 1])

    for k in range(1, 8):
        first_y(k).start()
        first_z(k).start()

    def tail_in(i):
        return remote(tin.at[i], tin.at[i], ts.at[i], tr.at[i], other)

    def x_copy(i):
        k = i % 4 + 1
        return remote(out.at[i], fin.at[i // 4, k - 1], xs.at[i], xr.at[i], x_peers[k - 1])

    def pass_block(i):
        tail_in(i).wait_recv()
        out[i] = hg[tail_block(i, q)] + tin[i]
        if i % 4 < 3:
            x_copy(i).start()

    def x_total(c):
        acc = out[4 * c + 3]
        for k in range(3):
            x_copy(4 * c + k).wait_recv()
            acc = acc + fin[c, k]
        return acc

    for i in range(4):
        pass_block(i)

    all_of(sy, rys, ryr).wait_recv()
    acc = p[chunk(y), :]
    for k in range(7):
        acc = acc + sy[k]
    fy[0] = acc

    def second_z(k):
        return remote(fy.at[0], fy.at[k], bzs, bzr, z_peers[k - 1])

    for k in range(1, 8):
        second_z(k).start()
    all_of(sz, rzs, rzr).wait_recv()
    acc = p[chunk(z, 128), :]
    for k in range(7):
        acc = acc + sz[k]
    fz[0] = acc

    def second_y(k):
        return remote(fz.at[0], fz.at[k], bys, byr, y_peers[k - 1])

    for k in range(1, 8):
        second_y(k).start()

    pass_block(4)
    pass_block(5)
    ysend[...] = x_total(0)
    along_y = remote(ysend, yrecv, ps, pr, pair)
    along_y.start()
    pass_block(6)
    pass_block(7)

    all_of(fy.at[pl.ds(1, 7)], bzs, bzr).wait_recv()
    acc = fy[(z + 8) % 8]
    for i in range(1, 8):
        acc = acc + fy[(z - i + 8) % 8]
    slab = x * 256
    at_y = pl.ds(pl.multiple_of(slab + y * 16, 16), 16)
    full[at_y, :] = acc

    def third_y(k):
        return remote(full.at[at_y], full.at[at_y], ays.at[k - 1], ayr.at[k - 1], y_peers[k - 1])

    def third_y_in(k):
        src = pl.ds(pl.multiple_of(slab + ((y - k + 8) % 8) * 16, 16), 16)
        return remote(full.at[src], full.at[src], ays.at[k - 1], ayr.at[k - 1], y_peers[k - 1])

    for k in range(1, 8):
        third_y(k).start()
    all_of(fz.at[pl.ds(1, 7)], bys, byr).wait_recv()
    acc = fz[(y + 8) % 8]
    for i in range(1, 8):
        acc = acc + fz[(y - i + 8) % 8]
    at_z = pl.ds(pl.multiple_of(slab + 128 + z * 16, 16), 16)
    full[at_z, :] = acc

    def third_z(k):
        return remote(full.at[at_z], full.at[at_z], azs.at[k - 1], azr.at[k - 1], z_peers[k - 1])

    def third_z_in(k):
        src = pl.ds(pl.multiple_of(slab + 128 + ((z - k + 8) % 8) * 16, 16), 16)
        return remote(full.at[src], full.at[src], azs.at[k - 1], azr.at[k - 1], z_peers[k - 1])

    for k in range(1, 8):
        third_z(k).start()

    def half(xx, h):
        return pl.ds(pl.multiple_of(xx * 256 + h * 128, 128), 128)

    def gather_x(k, h, n):
        at = pl.ds(pl.multiple_of(slab + h * 128 + n * 16, 16), 16)
        return remote(full.at[at], full.at[at], gxs.at[h, k - 1], gxr.at[h, k - 1], x_peers[k - 1])

    def gather_x_all(k, h):
        at = full.at[half((x - k + 4) % 4, h)]
        return remote(at, at, gxs.at[h, k - 1], gxr.at[h, k - 1], x_peers[k - 1])

    def swap(k, h):
        at = half((x - k + 4) % 4, h)
        return remote(full.at[at], peer.at[at], gcs.at[h, k], gcr.at[h, k], other)

    def spread(h, n):
        for k in (1, 3, 2):
            gather_x(k, h, n).start()

    spread(0, y)
    spread(1, z)
    for k in (1, 7, 2, 6, 3, 5, 4):
        third_y_in(k).wait_recv()
        spread(0, (y - k + 8) % 8)
        third_z_in(k).wait_recv()
        spread(1, (z - k + 8) % 8)
    swap(0, 0).start()
    swap(0, 1).start()
    ent[...] = x_total(1)
    along_y.wait_recv()
    ent[...] += yrecv[...]

    for h in range(2):
        for k in range(1, 4):
            gather_x_all(k, h).wait_recv()
            swap(k, h).start()

    n = rel.shape[0]

    @pl.when(is_head)
    def _():
        rel[:, 0:128] = full[0:n, :]

    @pl.when(is_next)
    def _():
        rel[:, 128:256] = full[0:n, :]

    for h in range(2):
        for k in range(4):
            swap(k, h).wait_recv()

    @pl.when(is_head)
    def _():
        rel[:, 128:256] = peer[0:n, :]

    @pl.when(is_next)
    def _():
        rel[:, 0:128] = peer[0:n, :]

    seven.wait_send()
    for i in range(8):
        tail_in(i).wait_send()
        if i % 4 < 3:
            x_copy(i).wait_send()
    for k in range(1, 8):
        third_y(k).wait_send()
        third_z(k).wait_send()
    all_of(sy, rys, ryr).wait_send()
    all_of(sz, rzs, rzr).wait_send()
    all_of(fy.at[pl.ds(1, 7)], bzs, bzr).wait_send()
    all_of(fz.at[pl.ds(1, 7)], bys, byr).wait_send()
    along_y.wait_send()
    for h in range(2):
        for k in range(1, 4):
            gather_x_all(k, h).wait_send()
        for k in range(4):
            swap(k, h).wait_send()


def reduce(hg, tg, listed, relations):
    whole = pl.BlockSpec(memory_space=VMEM)
    dma = pltpu.SemaphoreType.DMA
    rows = listed.shape[1]
    return pl.pallas_call(
        reduce_kernel,
        name="reduce_gradients",
        out_shape=(jax.ShapeDtypeStruct((BLOCK, WIDTH), F32), jax.ShapeDtypeStruct((relations, WIDTH), F32)),
        in_specs=[whole] * 3,
        out_specs=(whole, whole),
        scratch_shapes=[
            VMEM((8, rows, 128), F32),
            VMEM((BLOCKS, BLOCK, WIDTH), F32),
            VMEM((BLOCKS, BLOCK, WIDTH), F32),
            VMEM((2, 3, BLOCK, WIDTH), F32),
            VMEM((BLOCK, WIDTH), F32),
            VMEM((BLOCK, WIDTH), F32),
            VMEM((256, 128), F32),
            VMEM((7, 16, 128), F32),
            VMEM((7, 16, 128), F32),
            VMEM((8, 16, 128), F32),
            VMEM((8, 16, 128), F32),
            VMEM((REL_PAD, 128), F32),
            VMEM((REL_PAD, 128), F32),
            dma, dma,
            dma((8,)), dma((8,)),
            dma((8,)), dma((8,)),
            dma, dma,
            *[dma] * 8,
            *[dma((7,))] * 4,
            dma((2, 3)), dma((2, 3)),
            dma((2, 4)), dma((2, 4)),
        ],
        compiler_params=pltpu.CompilerParams(collective_id=1, has_side_effects=True, vmem_limit_bytes=40 << 20),
    )(hg, tg, listed)


def local(entity, rel_weight, tile_rel, tile_head, tile_tail, tile_mask, negatives, tile_count):
    ready = gather(entity, rel_weight, negatives, tile_mask, tile_rel, tile_head, tile_tail)
    hg, tg, listed = terms(*ready, tile_count)
    return reduce(hg, tg, listed, rel_weight.shape[0])


def solution(mesh):
    return jax.shard_map(
        local,
        mesh=mesh,
        in_specs=(
            P(("shard", "rep"), None),
            P(),
            P(("shard", "rep")),
            P(("shard", "rep")),
            P(("shard", "rep")),
            P(("shard", "rep"), None, None),
            P(("shard", "rep"), None),
            P(("shard", "rep")),
        ),
        out_specs=(P(("shard", "rep"), None), P()),
        check_vma=False,
    )
```

time: 736 us -> 111 us (0.15)
  waiting for transfers between devices: 471 us -> 0 us
  starting transfers between devices: 143 us -> 0 us
  Pallas kernels: 0 us -> 108 us
  other arithmetic: 46.3 us -> 0 us
  local copies, waits for them, and re-layouts: 30.8 us -> 1.58 us
  matrix products: 27 us -> 0 us
  between operations: 14.5 us -> 1.3 us
    psum x1 -> x0, waiting for transfers between devices: 293 us -> none  [local(): rel_total = lax.psum(rel_grad, ('shard', 'rep'))]
    ppermute x2 -> x0, starting transfers between devices: 143 us -> none  [shifted(): return lax.ppermute(block, axis, route)]
    pallas_call x0 -> x3, Pallas kernels: none -> 108 us  [the longest x1 50.7 us: reduce(): pl.pallas_call(reduce_kernel, name='reduce_gradients', out_shape=(jax.Sha...]
    reduce_scatter x1 -> x0, waiting for transfers between devices: 91.3 us -> none  [local(): lax.psum_scatter(head_grad + returned, 'rep', scatter_dimension=0, tiled=...]
    all_gather x1 -> x0, waiting for transfers between devices: 72.7 us -> none  [local(): head = lax.all_gather(entity, 'rep', axis=0, tiled=True)]
    scatter-add x12 -> x0, other arithmetic: 39.3 us -> none  [the longest x3 20.8 us: step(): tail_grad = tail_grad.at[negs.reshape(-1)].add(dneg.reshape(-1, width))]
    dot_general x18 -> x0, matrix products: 27 us -> none  [the longest x3 7.67 us: step(): negsc = jnp.einsum('tik,tjk->tij', scaled, nrows, precision=high)]
    gather x12 -> x0, local copies, waits for them, and re-layouts: 26.4 us -> none  [the longest x3 14 us: step(): nrows = tail[negs]]
  transfers between devices with their start and end apart: 5 -> 0, of which waited for: 5 -> 0; matrix products, arithmetic and copies ran while one was open for 0% -> 0% of each run, Pallas kernels for 0% -> 0%
where the time goes in v2:
time: 111 us
  Pallas kernels  108 us (97%)
  local copies, waits for them, and re-layouts  1.58 us (1%)
  between operations  1.3 us (1%)
    pallas_call x1, Pallas kernels, reduce(): pl.pallas_call(reduce_kernel, name='reduce_gradients', out_shape=(jax.Sha...  50.7 us
    pallas_call x1, Pallas kernels, gather(): pl.pallas_call(gather_kernel, name='gather_partitions', out_shape=(part,...  36.9 us
    pallas_call x1, Pallas kernels, terms(): pl.pallas_call(terms_kernel, name='tile_terms', out_shape=(part, part, ja...  20.2 us

profile of v2, /device:TPU:1, one launch (start us, length us, event | category | flops | bytes accessed | tf_op | source)
XLA Modules:
  0.0 110.7 jit_solution(627905290020674628)
XLA Ops:
  1.3 36.9 %gather_partitions.1 = (f32[8,128,256]{2,1,0:T(8,128)S(1)}, f32[8,128,256]{2,1,0:T(8,128)S(1)}, f32[900,256]{1,0:T(8,128)S(1)}, s32[32,256]{1,0:T(8,128)S(1)}, s...) custom-call(f32[128,256]{1,0:T(8,128)} %own_ref.1, f32[900,256]{1,0:T(8,128)} %relw_in.1, ...), custom_call_target="tpu_custom_call" | custom-call | tf_op jit(solution)/shard_map/gather_partitions/pallas_call | solution.py:220
  38.2 20.2 %tile_terms.1 = (f32[8,128,256]{2,1,0:T(8,128)S(1)}, f32[8,128,256]{2,1,0:T(8,128)S(1)}, f32[2,40,128]{2,1,0:T(8,128)S(1)}) custom-call(s32[32]{0:T(128)S(1)} %get-tuple-element.13.rel_s, s32[32]{0:T(128)S(1)} %get-tuple-element.14.head_s, s32[32]{0:T(128)S(1)} %get-tuple-element.15.tail_s, s32[1]{0:T(128)S(6)} %copy.12.count_s, ...), custom_call_target="tpu_custom_call" | custom-call | tf_op jit(solution)/shard_map/tile_terms/pallas_call | solution.py:355
  58.4 50.7 %reduce_gradients.1 = (f32[128,256]{1,0:T(8,128)S(1)}, f32[900,256]{1,0:T(8,128)S(1)}) custom-call(f32[8,128,256]{2,1,0:T(8,128)S(1)} %get-tuple-element.21.hg, f32[8,128,256]{2,1,0:T(8,128)S(1)} %get-tuple-element.22.tg, f32[2,40,128]{2,1,0:T(8,128)S(1)} %get-tuple-element.23.listed), custom_call_target="tpu_custom_call" | custom-call | tf_op jit(solution)/shard_map/reduce_gradients/pallas_call | solution.py:641
  109.1 0.7 copy.13
  109.8 0.9 copy.14

commit v3 on v2

--- a/solution.py
+++ b/solution.py
@@ -49,10 +49,16 @@
     )
 
 
+def halves(value):
+    hi = value.astype(BF16)
+    lo = (value - hi.astype(F32)).astype(BF16)
+    return hi, lo
+
+
 def gather_kernel(
     own_ref, relw_in, negs_in, mask_in, rel_in, head_in, tail_in,
-    head, tail, relw, negs, mask, rel_s, head_s, tail_s,
-    ys, yr, xs, xr, cs, cr, ls, ms,
+    head, t_cols, t_rows, relw, negs, mask, rel_s, head_s, tail_s,
+    tail, ys, yr, xs, xr, cs, cr, ls, ms,
 ):
     x, y, z, core = place()
     brought = [(relw_in, relw), (negs_in, negs), (mask_in, mask), (rel_in, rel_s), (head_in, head_s), (tail_in, tail_s)]
@@ -128,6 +134,16 @@
     def across_in(n):
         return remote(tail.at[shared[n]], tail.at[shared[n]], cs.at[n], cr.at[n], other)
 
+    def split(block):
+        hi, lo = halves(tail[block])
+        at = pl.ds(pl.multiple_of(block * BLOCK, BLOCK), BLOCK)
+        t_cols[at, 0:256] = hi
+        t_cols[at, 256:512] = hi
+        t_cols[at, 512:768] = lo
+        n, sub = block // 2, (block % 2) * BLOCK
+        for k, part in enumerate((hi, hi, lo)):
+            t_rows[n, pl.ds(pl.multiple_of(k * 256 + sub, BLOCK), BLOCK), :] = part
+
     @pl.when(is_next)
     def _():
         near_copy.start()
@@ -176,14 +192,21 @@
 
     @pl.when(is_head)
     def _():
-        for i in (1, 4, 5):
-            for k in range(1, 4):
-                from_x(i, k).wait_recv()
+        split(2 * x + q_near)
+        split(2 * x + 1 - q_near)
+        for k in (1, 3, 2):
+            from_x(1, k).wait_recv()
+            split(2 * ((x - k + 4) % 4) + q_near)
+        for k in (1, 3, 2):
+            from_x(4, k).wait_recv()
+            from_x(5, k).wait_recv()
+            split(2 * ((x - k + 4) % 4) + 1 - q_near)
 
     @pl.when(is_next)
     def _():
         for n in range(8):
             across_in(n).wait_recv()
+            split(shared[n])
 
     keep.wait()
     for c in local_copies:
@@ -220,27 +243,29 @@
     return pl.pallas_call(
         gather_kernel,
         name="gather_partitions",
-        out_shape=(part, part, *[jax.ShapeDtypeStruct(a.shape, a.dtype) for a in operands[1:]]),
+        out_shape=(
+            part,
+            jax.ShapeDtypeStruct((BLOCKS * BLOCK, 3 * WIDTH), BF16),
+            jax.ShapeDtypeStruct((4, 3 * WIDTH, WIDTH), BF16),
+            *[jax.ShapeDtypeStruct(a.shape, a.dtype) for a in operands[1:]],
+        ),
         in_specs=[hbm] * 7,
-        out_specs=(whole, whole, whole, whole, whole, scalars, scalars, scalars),
-        scratch_shapes=[dma((5,)), dma((5,)), dma((6, 3)), dma((6, 3)), dma((8,)), dma((8,)), dma, dma((6,))],
+        out_specs=(whole,) * 6 + (scalars,) * 3,
+        scratch_shapes=[
+            VMEM((BLOCKS, BLOCK, WIDTH), F32),
+            dma((5,)), dma((5,)), dma((6, 3)), dma((6, 3)), dma((8,)), dma((8,)), dma, dma((6,)),
+        ],
         compiler_params=pltpu.CompilerParams(collective_id=0, has_side_effects=True, vmem_limit_bytes=32 << 20),
     )(*operands)
 
 
-def halves(value):
-    hi = value.astype(BF16)
-    lo = (value - hi.astype(F32)).astype(BF16)
-    return hi, lo
-
-
 def dot_nt(a, b):
     return lax.dot_general(a, b, (((1,), (1,)), ((), ())), preferred_element_type=F32)
 
 
 def terms_kernel(
-    rel_s, head_s, tail_s, count_s, head, tail, relw, negs, mask, hgrad, tgrad, listed,
-    t_cols, t_rows, xx, xt, scores, g_hi, g_lo, mixed, tg_t, counts,
+    rel_s, head_s, tail_s, count_s, head, t_cols, t_rows, relw, negs, mask, hgrad, tgrad, listed,
+    xx, xt, scores, g_hi, g_lo, mixed, counts,
 ):
     count = count_s[0]
     parts = 4
@@ -250,17 +275,7 @@
 
     hgrad[...] = jnp.zeros_like(hgrad)
     listed[...] = jnp.zeros_like(listed)
-    tg_t[...] = jnp.zeros_like(tg_t)
-    for b in range(BLOCKS):
-        hi, lo = halves(tail[b])
-        at = pl.ds(b * BLOCK, BLOCK)
-        t_cols[at, 0:256] = hi
-        t_cols[at, 256:512] = hi
-        t_cols[at, 512:768] = lo
-        n, sub = b // 2, (b % 2) * BLOCK
-        t_rows[n, pl.ds(sub, BLOCK), :] = hi
-        t_rows[n, pl.ds(256 + sub, BLOCK), :] = hi
-        t_rows[n, pl.ds(512 + sub, BLOCK), :] = lo
+    tgrad[...] = jnp.zeros_like(tgrad)
 
     lane = lax.broadcasted_iota(jnp.int32, (8, 128), 1) % tiles
     ids = jnp.zeros((8, 128), F32)
@@ -312,7 +327,9 @@
 
         def make_tail(n):
             weights = jnp.concatenate([g_hi[n], g_hi[n], g_lo[n]], axis=0)
-            tg_t[:, pl.ds(n * step, step)] += jnp.dot(xt[...], weights, preferred_element_type=F32)
+            part = jnp.dot(xt[...], weights, preferred_element_type=F32)
+            tgrad[n, 0] += part[:, 0:BLOCK]
+            tgrad[n, 1] += part[:, BLOCK:]
 
         def make_mixed(n):
             rows_in = jnp.concatenate([g_hi[n], g_lo[n], g_hi[n]], axis=1)
@@ -342,11 +359,9 @@
         return carry
 
     lax.fori_loop(0, (count + GROUP - 1) // GROUP, do_group, 0)
-    for b in range(BLOCKS):
-        tgrad[b] = tg_t[:, pl.ds(b * BLOCK, BLOCK)].T
-
-
-def terms(head, tail, relw, negs, mask, rel_s, head_s, tail_s, count_s):
+
+
+def terms(head, t_cols, t_rows, relw, negs, mask, rel_s, head_s, tail_s, count_s):
     rows = GROUP * BLOCK
     tiles = mask.shape[0]
     whole = pl.BlockSpec(memory_space=VMEM)
@@ -355,29 +370,26 @@
     return pl.pallas_call(
         terms_kernel,
         name="tile_terms",
-        out_shape=(part, part, jax.ShapeDtypeStruct((2, tiles + 8, 128), F32)),
-        in_specs=[scalars] * 4 + [whole] * 5,
+        out_shape=(part, jax.ShapeDtypeStruct((4, 2, WIDTH, BLOCK), F32), jax.ShapeDtypeStruct((2, tiles + 8, 128), F32)),
+        in_specs=[scalars] * 4 + [whole] * 6,
         out_specs=(whole, whole, whole),
         scratch_shapes=[
-            VMEM((BLOCKS * BLOCK, 3 * WIDTH), BF16),
-            VMEM((4, 3 * WIDTH, WIDTH), BF16),
             VMEM((rows, 3 * WIDTH), BF16),
             VMEM((WIDTH, 3 * rows), BF16),
             VMEM((4, rows, WIDTH), F32),
             VMEM((4, rows, WIDTH), BF16),
             VMEM((4, rows, WIDTH), BF16),
             VMEM((rows, WIDTH), F32),
-            VMEM((WIDTH, BLOCKS * BLOCK), F32),
             VMEM((GROUP, BLOCKS, BLOCK), F32),
         ],
         compiler_params=pltpu.CompilerParams(vmem_limit_bytes=40 << 20),
-    )(rel_s, head_s, tail_s, count_s, head, tail, relw, negs, mask)
+    )(rel_s, head_s, tail_s, count_s, head, t_cols, t_rows, relw, negs, mask)
 
 
 def reduce_kernel(
     hg, tg, listed, ent, rel,
-    lists, tin, out, fin, ysend, yrecv, p, sy, sz, fy, fz, full, peer,
-    ls, lr, ts, tr, xs, xr, ps, pr, rys, ryr, rzs, rzr, bys, byr, bzs, bzr, ays, ayr, azs, azr, gxs, gxr, gcs, gcr,
+    lists, tin, out, fin, tfin, tsend, trecv, ysend, yrecv, p, sz, fz, full, peer,
+    ls, lr, ts, tr, xs, xr, us, ur, vs, vr, ps, pr, rzs, rzr, bys, byr, azs, azr, gxs, gxr, gcs, gcr,
 ):
     x, y, z, core = place()
     q = y // 4
@@ -388,12 +400,13 @@
     y_peers = [device(x, y + k, z, core) for k in range(1, 8)]
     z_peers = [device(x, y, z + k, core) for k in range(1, 8)]
     y_lo = y % 4
-    down = device(x, y - 1, z - (3 - y_lo) // 3, 1)
-    up = device(x, y + 1, z + y_lo // 3, 0)
+    sign = 2 * core - 1
+    z_there = z + core * (y_lo // 3) - (1 - core) * ((3 - y_lo) // 3)
+    near_dev = device(x, y + sign, z_there, 1 - core)
+    far_dev = device(x, y + 5 * sign, z_there, 1 - core)
     is_head = core == 0
     is_next = core == 1
-    chain_dev = device(x, y + 2 * core - 1, z + core * (y_lo // 3) - (1 - core) * ((3 - y_lo) // 3), 1 - core)
-    greet(x_peers + x_over + y_peers + z_peers + [other, chain_dev])
+    greet(x_peers + x_over + y_peers + z_peers + [other, near_dev, far_dev])
     me = core * 4 + x
     tiles = listed.shape[1] - 8
 
@@ -409,25 +422,34 @@
         list_copy(i).start()
     lists[me] = listed[core]
 
-    def tail_block(i, q_of):
-        parity = 1 - q_of if i < 4 else q_of
-        return 2 * ((x + 1 + i % 4) % 4) + parity
-
+    to_other = remote(tg, tin, ts, tr, other)
     q_down = ((y + 7) % 8) // 4
 
-    def tail_copy(i, q_of, target):
-        block = tail_block(i, q_of)
-        return remote(tg.at[block], tin.at[i], ts.at[i], tr.at[i], target)
-
-    @pl.when(is_head)
-    def _():
-        for i in range(8):
-            tail_copy(i, q_down, down).start()
-
-    @pl.when(is_next)
-    def _():
-        for i in range(8):
-            tail_copy(i, q, other).start()
+    def tail_x(k):
+        return remote(tg.at[(x + k) % 4], tfin.at[k - 1], us.at[k - 1], ur.at[k - 1], x_peers[k - 1])
+
+    def head_block(i):
+        return 2 * ((x + 1 + i % 4) % 4) + (1 - q if i < 4 else q)
+
+    def head_x(i, src):
+        k = i % 4 + 1
+        return remote(src, fin.at[i // 4, k - 1], xs.at[i], xr.at[i], x_peers[k - 1])
+
+    def tail_y(c, target):
+        return remote(tsend.at[c], trecv.at[c], vs.at[c], vr.at[c], target)
+
+    sent_blocks = (0, 2, 1, 4, 6, 5)
+
+    @pl.when(is_head)
+    def _():
+        for k in (1, 3, 2):
+            tail_x(k).start()
+
+    @pl.when(is_next)
+    def _():
+        to_other.start()
+        for i in sent_blocks:
+            head_x(i, hg.at[head_block(i)]).start()
 
     seven = remote(lists.at[pl.ds(0, 7)], lists.at[pl.ds(0, 7)], ls, lr, other)
     seven.wait_recv()
@@ -451,187 +473,156 @@
     placed = placed + jnp.dot(chosen, low, preferred_element_type=F32)
     p[...] = placed
 
-    def chunk(k, base=0):
-        return pl.ds(pl.multiple_of(base + k * 16, 16), 16)
+    def chunk(k):
+        return pl.ds(pl.multiple_of(k * 32, 32), 32)
 
     def all_of(buffer, send, recv):
         return remote(buffer, buffer, send, recv, other)
 
-    def first_y(k):
-        return remote(p.at[chunk((y + k) % 8)], sy.at[k - 1], rys, ryr, y_peers[k - 1])
-
-    def first_z(k):
-        return remote(p.at[chunk((z + k) % 8, 128)], sz.at[k - 1], rzs, rzr, z_peers[k - 1])
-
     for k in range(1, 8):
-        first_y(k).start()
-        first_z(k).start()
-
-    def tail_in(i):
-        return remote(tin.at[i], tin.at[i], ts.at[i], tr.at[i], other)
-
-    def x_copy(i):
-        k = i % 4 + 1
-        return remote(out.at[i], fin.at[i // 4, k - 1], xs.at[i], xr.at[i], x_peers[k - 1])
-
-    def pass_block(i):
-        tail_in(i).wait_recv()
-        out[i] = hg[tail_block(i, q)] + tin[i]
-        if i % 4 < 3:
-            x_copy(i).start()
+        remote(p.at[chunk((z + k) % 8)], sz.at[k - 1], rzs, rzr, z_peers[k - 1]).start()
+
+    @pl.when(is_head)
+    def _():
+        to_other.wait_recv()
+        for i in sent_blocks + (3, 7):
+            block = head_block(i)
+            out[i] = hg[block] + tin[block // 2, block % 2].T
+            if i % 4 < 3:
+                head_x(i, out.at[i]).start()
+
+    @pl.when(is_next)
+    def _():
+        for i in (3, 7):
+            out[i] = hg[head_block(i)]
 
     def x_total(c):
         acc = out[4 * c + 3]
         for k in range(3):
-            x_copy(4 * c + k).wait_recv()
+            head_x(4 * c + k, out.at[4 * c + k]).wait_recv()
             acc = acc + fin[c, k]
         return acc
 
-    for i in range(4):
-        pass_block(i)
-
-    all_of(sy, rys, ryr).wait_recv()
-    acc = p[chunk(y), :]
-    for k in range(7):
-        acc = acc + sy[k]
-    fy[0] = acc
-
-    def second_z(k):
-        return remote(fy.at[0], fy.at[k], bzs, bzr, z_peers[k - 1])
-
-    for k in range(1, 8):
-        second_z(k).start()
     all_of(sz, rzs, rzr).wait_recv()
-    acc = p[chunk(z, 128), :]
+    acc = p[chunk(z), :]
     for k in range(7):
         acc = acc + sz[k]
     fz[0] = acc
-
-    def second_y(k):
-        return remote(fz.at[0], fz.at[k], bys, byr, y_peers[k - 1])
-
     for k in range(1, 8):
-        second_y(k).start()
-
-    pass_block(4)
-    pass_block(5)
-    ysend[...] = x_total(0)
-    along_y = remote(ysend, yrecv, ps, pr, pair)
-    along_y.start()
-    pass_block(6)
-    pass_block(7)
-
-    all_of(fy.at[pl.ds(1, 7)], bzs, bzr).wait_recv()
-    acc = fy[(z + 8) % 8]
-    for i in range(1, 8):
-        acc = acc + fy[(z - i + 8) % 8]
-    slab = x * 256
-    at_y = pl.ds(pl.multiple_of(slab + y * 16, 16), 16)
-    full[at_y, :] = acc
-
-    def third_y(k):
-        return remote(full.at[at_y], full.at[at_y], ays.at[k - 1], ayr.at[k - 1], y_peers[k - 1])
-
-    def third_y_in(k):
-        src = pl.ds(pl.multiple_of(slab + ((y - k + 8) % 8) * 16, 16), 16)
-        return remote(full.at[src], full.at[src], ays.at[k - 1], ayr.at[k - 1], y_peers[k - 1])
-
-    for k in range(1, 8):
-        third_y(k).start()
+        remote(fz.at[0], fz.at[k], bys, byr, y_peers[k - 1]).start()
+
+    @pl.when(is_head)
+    def _():
+        for k in range(1, 4):
+            tail_x(k).wait_recv()
+        for c, parity in ((0, q_down), (1, 1 - q_down)):
+            tsend[c] = tg[x, parity] + tfin[0, parity] + tfin[1, parity] + tfin[2, parity]
+        tail_y(0, near_dev).start()
+        tail_y(1, far_dev).start()
+
+
     all_of(fz.at[pl.ds(1, 7)], bys, byr).wait_recv()
     acc = fz[(y + 8) % 8]
     for i in range(1, 8):
         acc = acc + fz[(y - i + 8) % 8]
-    at_z = pl.ds(pl.multiple_of(slab + 128 + z * 16, 16), 16)
+    slab = x * 256
+    at_z = pl.ds(pl.multiple_of(slab + z * 32, 32), 32)
     full[at_z, :] = acc
 
     def third_z(k):
         return remote(full.at[at_z], full.at[at_z], azs.at[k - 1], azr.at[k - 1], z_peers[k - 1])
 
     def third_z_in(k):
-        src = pl.ds(pl.multiple_of(slab + 128 + ((z - k + 8) % 8) * 16, 16), 16)
+        src = pl.ds(pl.multiple_of(slab + ((z - k + 8) % 8) * 32, 32), 32)
         return remote(full.at[src], full.at[src], azs.at[k - 1], azr.at[k - 1], z_peers[k - 1])
 
     for k in range(1, 8):
         third_z(k).start()
 
-    def half(xx, h):
-        return pl.ds(pl.multiple_of(xx * 256 + h * 128, 128), 128)
-
-    def gather_x(k, h, n):
-        at = pl.ds(pl.multiple_of(slab + h * 128 + n * 16, 16), 16)
-        return remote(full.at[at], full.at[at], gxs.at[h, k - 1], gxr.at[h, k - 1], x_peers[k - 1])
-
-    def gather_x_all(k, h):
-        at = full.at[half((x - k + 4) % 4, h)]
-        return remote(at, at, gxs.at[h, k - 1], gxr.at[h, k - 1], x_peers[k - 1])
-
-    def swap(k, h):
-        at = half((x - k + 4) % 4, h)
-        return remote(full.at[at], peer.at[at], gcs.at[h, k], gcr.at[h, k], other)
-
-    def spread(h, n):
+    ysend[...] = x_total(0)
+    along_y = remote(ysend, yrecv, ps, pr, pair)
+    along_y.start()
+
+    def whole(xx):
+        return pl.ds(pl.multiple_of(xx * 256, 256), 256)
+
+    def spread(n):
+        at = full.at[pl.ds(pl.multiple_of(slab + n * 32, 32), 32)]
         for k in (1, 3, 2):
-            gather_x(k, h, n).start()
-
-    spread(0, y)
-    spread(1, z)
+            remote(at, at, gxs.at[k - 1], gxr.at[k - 1], x_peers[k - 1]).start()
+
+    def gather_x_all(k):
+        at = full.at[whole((x - k + 4) % 4)]
+        return remote(at, at, gxs.at[k - 1], gxr.at[k - 1], x_peers[k - 1])
+
+    def swap(k):
+        at = whole((x - k + 4) % 4)
+        return remote(full.at[at], peer.at[at], gcs.at[k], gcr.at[k], other)
+
+    spread(z)
     for k in (1, 7, 2, 6, 3, 5, 4):
-        third_y_in(k).wait_recv()
-        spread(0, (y - k + 8) % 8)
         third_z_in(k).wait_recv()
-        spread(1, (z - k + 8) % 8)
-    swap(0, 0).start()
-    swap(0, 1).start()
+        spread((z - k + 8) % 8)
+    swap(0).start()
     ent[...] = x_total(1)
     along_y.wait_recv()
     ent[...] += yrecv[...]
 
-    for h in range(2):
+    @pl.when(is_next)
+    def _():
+        for c in range(2):
+            tail_y(c, near_dev).wait_recv()
+        ent[...] += (trecv[0] + trecv[1]).T
+
+    for k in (1, 3, 2):
+        gather_x_all(k).wait_recv()
+        swap(k).start()
+
+    n = rel.shape[0]
+
+    @pl.when(is_head)
+    def _():
+        rel[:, 0:128] = full[0:n, :]
+
+    @pl.when(is_next)
+    def _():
+        rel[:, 128:256] = full[0:n, :]
+
+    for k in range(4):
+        swap(k).wait_recv()
+
+    @pl.when(is_head)
+    def _():
+        rel[:, 128:256] = peer[0:n, :]
+
+    @pl.when(is_next)
+    def _():
+        rel[:, 0:128] = peer[0:n, :]
+
+    seven.wait_send()
+    for i in sent_blocks:
+        head_x(i, out.at[i]).wait_send()
+
+    @pl.when(is_head)
+    def _():
         for k in range(1, 4):
-            gather_x_all(k, h).wait_recv()
-            swap(k, h).start()
-
-    n = rel.shape[0]
-
-    @pl.when(is_head)
-    def _():
-        rel[:, 0:128] = full[0:n, :]
-
-    @pl.when(is_next)
-    def _():
-        rel[:, 128:256] = full[0:n, :]
-
-    for h in range(2):
-        for k in range(4):
-            swap(k, h).wait_recv()
-
-    @pl.when(is_head)
-    def _():
-        rel[:, 128:256] = peer[0:n, :]
-
-    @pl.when(is_next)
-    def _():
-        rel[:, 0:128] = peer[0:n, :]
-
-    seven.wait_send()
-    for i in range(8):
-        tail_in(i).wait_send()
-        if i % 4 < 3:
-            x_copy(i).wait_send()
+            tail_x(k).wait_send()
+        for c in range(2):
+            tail_y(c, near_dev).wait_send()
+
+    @pl.when(is_next)
+    def _():
+        to_other.wait_send()
+
     for k in range(1, 8):
-        third_y(k).wait_send()
         third_z(k).wait_send()
-    all_of(sy, rys, ryr).wait_send()
     all_of(sz, rzs, rzr).wait_send()
-    all_of(fy.at[pl.ds(1, 7)], bzs, bzr).wait_send()
     all_of(fz.at[pl.ds(1, 7)], bys, byr).wait_send()
     along_y.wait_send()
-    for h in range(2):
-        for k in range(1, 4):
-            gather_x_all(k, h).wait_send()
-        for k in range(4):
-            swap(k, h).wait_send()
+    for k in range(1, 4):
+        gather_x_all(k).wait_send()
+    for k in range(4):
+        swap(k).wait_send()
 
 
 def reduce(hg, tg, listed, relations):
@@ -646,26 +637,29 @@
         out_specs=(whole, whole),
         scratch_shapes=[
             VMEM((8, rows, 128), F32),
-            VMEM((BLOCKS, BLOCK, WIDTH), F32),
+            VMEM((4, 2, WIDTH, BLOCK), F32),
             VMEM((BLOCKS, BLOCK, WIDTH), F32),
             VMEM((2, 3, BLOCK, WIDTH), F32),
+            VMEM((3, 2, WIDTH, BLOCK), F32),
+            VMEM((2, WIDTH, BLOCK), F32),
+            VMEM((2, WIDTH, BLOCK), F32),
             VMEM((BLOCK, WIDTH), F32),
             VMEM((BLOCK, WIDTH), F32),
             VMEM((256, 128), F32),
-            VMEM((7, 16, 128), F32),
-            VMEM((7, 16, 128), F32),
-            VMEM((8, 16, 128), F32),
-            VMEM((8, 16, 128), F32),
+            VMEM((7, 32, 128), F32),
+            VMEM((8, 32, 128), F32),
             VMEM((REL_PAD, 128), F32),
             VMEM((REL_PAD, 128), F32),
             dma, dma,
+            dma, dma,
             dma((8,)), dma((8,)),
-            dma((8,)), dma((8,)),
+            dma((3,)), dma((3,)),
+            dma((2,)), dma((2,)),
             dma, dma,
-            *[dma] * 8,
-            *[dma((7,))] * 4,
-            dma((2, 3)), dma((2, 3)),
-            dma((2, 4)), dma((2, 4)),
+            dma, dma, dma, dma,
+            dma((7,)), dma((7,)),
+            dma((3,)), dma((3,)),
+            dma((4,)), dma((4,)),
         ],
         compiler_params=pltpu.CompilerParams(collective_id=1, has_side_effects=True, vmem_limit_bytes=40 << 20),
     )(hg, tg, listed)

time: 111 us -> 104 us (0.937)
  Pallas kernels: 108 us -> 101 us
    pallas_call x1, Pallas kernels: 20.2 us -> 13.4 us  [terms(): pl.pallas_call(terms_kernel, name='tile_terms', out_shape=(part, jax.Shap...]
where the time goes in v3:
time: 104 us
  Pallas kernels  101 us (97%)
  local copies, waits for them, and re-layouts  1.58 us (2%)
  between operations  1.3 us (1%)
    pallas_call x1, Pallas kernels, reduce(): pl.pallas_call(reduce_kernel, name='reduce_gradients', out_shape=(jax.Sha...  50.5 us
    pallas_call x1, Pallas kernels, gather(): pl.pallas_call(gather_kernel, name='gather_partitions', out_shape=(part,...  37 us
    pallas_call x1, Pallas kernels, terms(): pl.pallas_call(terms_kernel, name='tile_terms', out_shape=(part, jax.Shap...  13.4 us

profile of v3, /device:TPU:1, one launch (start us, length us, event | category | flops | bytes accessed | tf_op | source)
XLA Modules:
  0.0 103.7 jit_solution(9102184841772802042)
XLA Ops:
  1.3 37.0 %gather_partitions.1 = (f32[8,128,256]{2,1,0:T(8,128)S(1)}, bf16[1024,768]{1,0:T(8,128)(2,1)S(1)}, bf16[4,768,256]{2,1,0:T(8,128)(2,1)S(1)}, f32[900,256]{1,0:T(...) custom-call(f32[128,256]{1,0:T(8,128)} %own_ref.1, ...), custom_call_target="tpu_custom_call" | custom-call | tf_op jit(solution)/shard_map/gather_partitions/pallas_call | solution.py:243
  38.3 13.4 %tile_terms.1 = (f32[8,128,256]{2,1,0:T(8,128)S(1)}, f32[4,2,256,128]{3,2,1,0:T(8,128)S(1)}, f32[2,40,128]{2,1,0:T(8,128)S(1)}) custom-call(s32[32]{0:T(128)S(1)} %get-tuple-element.14.rel_s, s32[32]{0:T(128)S(1)} %get-tuple-element.15.head_s, s32[32]{0:T(128)S(1)} %get-tuple-element.16.tail_s, s32[1]{0:T(128)S(6)} %copy.12.count_s, ...), custom_call_target="tpu_custom_call" | custom-call | tf_op jit(solution)/shard_map/tile_terms/pallas_call | solution.py:370
  51.7 50.5 %reduce_gradients.1 = (f32[128,256]{1,0:T(8,128)S(1)}, f32[900,256]{1,0:T(8,128)S(1)}) custom-call(f32[8,128,256]{2,1,0:T(8,128)S(1)} %get-tuple-element.23.hg, f32[4,2,256,128]{3,2,1,0:T(8,128)S(1)} %get-tuple-element.24.tg, f32[2,40,128]{2,1,0:T(8,128)S(1)} %get-tuple-element.25.listed), custom_call_target="tpu_custom_call" | custom-call | tf_op jit(solution)/shard_map/reduce_gradients/pallas_call | solution.py:632
  102.1 0.7 copy.13
  102.8 0.9 copy.14

commit v4 on v3

--- a/solution.py
+++ b/solution.py
@@ -264,8 +264,8 @@
 
 
 def terms_kernel(
-    rel_s, head_s, tail_s, count_s, head, t_cols, t_rows, relw, negs, mask, hgrad, tgrad, listed,
-    xx, xt, scores, g_hi, g_lo, mixed, counts,
+    rel_s, head_s, tail_s, count_s, head, t_cols, t_rows, relw, negs, mask, hgrad, listed, xt, g_hi, g_lo,
+    xx, scores, mixed, counts, edges,
 ):
     count = count_s[0]
     parts = 4
@@ -275,7 +275,6 @@
 
     hgrad[...] = jnp.zeros_like(hgrad)
     listed[...] = jnp.zeros_like(listed)
-    tgrad[...] = jnp.zeros_like(tgrad)
 
     lane = lax.broadcasted_iota(jnp.int32, (8, 128), 1) % tiles
     ids = jnp.zeros((8, 128), F32)
@@ -294,9 +293,9 @@
             xx[at, 256:512] = lo
             xx[at, 512:768] = hi
             hi_t, lo_t = halves(scaled.T)
-            xt[:, pl.ds(j * BLOCK, BLOCK)] = hi_t
-            xt[:, pl.ds(rows + j * BLOCK, BLOCK)] = lo_t
-            xt[:, pl.ds(2 * rows + j * BLOCK, BLOCK)] = hi_t
+            xt[group, :, pl.ds(j * BLOCK, BLOCK)] = hi_t
+            xt[group, :, pl.ds(rows + j * BLOCK, BLOCK)] = lo_t
+            xt[group, :, pl.ds(2 * rows + j * BLOCK, BLOCK)] = hi_t
             live = (tile < count).astype(F32)
             drawn = negs[pl.ds(tile, 1), :]
             upper = (lax.broadcasted_iota(jnp.int32, (BLOCKS, 256), 0) == drawn // BLOCK).astype(F32)
@@ -306,46 +305,42 @@
         def make_scores(n):
             scores[n] = dot_nt(xx[...], t_cols[pl.ds(n * step, step), :])
 
+        def make_edges(j):
+            tile = group * GROUP + j
+            b = tail_s[tile]
+            at = pl.ds(pl.multiple_of((b % 2) * BLOCK, BLOCK), BLOCK)
+            own = scores[b // 2, pl.ds(j * BLOCK, BLOCK), at]
+            live = jnp.where(tile < count, 1.0, 0.0).astype(F32)
+            edges[j] = (mask[tile].astype(F32) * live) * lax.logistic(-own)
+
         def make_grads(n):
             for j in range(GROUP):
                 tile = group * GROUP + j
-                alive = tile < count
                 at = pl.ds(j * BLOCK, BLOCK)
-                marked = mask[tile].astype(F32)
                 for h in range(2):
                     b = 2 * n + h
-                    s = scores[n, at, h * BLOCK:(h + 1) * BLOCK]
-                    e = jnp.exp(-jnp.abs(s))
-                    big = 1.0 / (1.0 + e)
-                    small = e * big
-                    up = s >= 0.0
-                    here = jnp.where(jnp.logical_and(alive, tail_s[tile] == b), 1.0, 0.0).astype(F32)
-                    g = counts[j, b:b + 1, :] * jnp.where(up, big, small) - (marked * here) * jnp.where(up, small, big)
+                    lanes = slice(h * BLOCK, (h + 1) * BLOCK)
+                    here = jnp.where(tail_s[tile] == b, 1.0, 0.0).astype(F32)
+                    g = counts[j, b:b + 1, :] * lax.logistic(scores[n, at, lanes]) - here * edges[j]
                     hi, lo = halves(g)
-                    g_hi[n, at, h * BLOCK:(h + 1) * BLOCK] = hi
-                    g_lo[n, at, h * BLOCK:(h + 1) * BLOCK] = lo
-
-        def make_tail(n):
-            weights = jnp.concatenate([g_hi[n], g_hi[n], g_lo[n]], axis=0)
-            part = jnp.dot(xt[...], weights, preferred_element_type=F32)
-            tgrad[n, 0] += part[:, 0:BLOCK]
-            tgrad[n, 1] += part[:, BLOCK:]
+                    g_hi[group, n, at, lanes] = hi
+                    g_lo[group, n, at, lanes] = lo
 
         def make_mixed(n):
-            rows_in = jnp.concatenate([g_hi[n], g_lo[n], g_hi[n]], axis=1)
+            rows_in = jnp.concatenate([g_hi[group, n], g_lo[group, n], g_hi[group, n]], axis=1)
             part = jnp.dot(rows_in, t_rows[n], preferred_element_type=F32)
             if n == 0:
                 mixed[...] = part
             else:
                 mixed[...] += part
 
-        make_scores(0)
         for n in range(parts):
-            if n + 1 < parts:
-                make_scores(n + 1)
+            make_scores(n)
+        for j in range(GROUP):
+            make_edges(j)
+        for n in range(parts):
             make_grads(n)
             make_mixed(n)
-            make_tail(n)
 
         for j in range(GROUP):
             tile = group * GROUP + j
@@ -358,7 +353,15 @@
             listed[1, pl.ds(tile, 1), :] = row[:, 128:256]
         return carry
 
-    lax.fori_loop(0, (count + GROUP - 1) // GROUP, do_group, 0)
+    def no_group(group, carry):
+        xt[group] = jnp.zeros(xt.shape[1:], BF16)
+        g_hi[group] = jnp.zeros(g_hi.shape[1:], BF16)
+        g_lo[group] = jnp.zeros(g_lo.shape[1:], BF16)
+        return carry
+
+    used = (count + GROUP - 1) // GROUP
+    lax.fori_loop(0, used, do_group, 0)
+    lax.fori_loop(used, tiles // GROUP, no_group, 0)
 
 
 def terms(head, t_cols, t_rows, relw, negs, mask, rel_s, head_s, tail_s, count_s):
@@ -370,25 +373,29 @@
     return pl.pallas_call(
         terms_kernel,
         name="tile_terms",
-        out_shape=(part, jax.ShapeDtypeStruct((4, 2, WIDTH, BLOCK), F32), jax.ShapeDtypeStruct((2, tiles + 8, 128), F32)),
+        out_shape=(
+            part,
+            jax.ShapeDtypeStruct((2, tiles + 8, 128), F32),
+            jax.ShapeDtypeStruct((tiles // GROUP, WIDTH, 3 * rows), BF16),
+            jax.ShapeDtypeStruct((tiles // GROUP, 4, rows, WIDTH), BF16),
+            jax.ShapeDtypeStruct((tiles // GROUP, 4, rows, WIDTH), BF16),
+        ),
         in_specs=[scalars] * 4 + [whole] * 6,
-        out_specs=(whole, whole, whole),
+        out_specs=(whole,) * 5,
         scratch_shapes=[
             VMEM((rows, 3 * WIDTH), BF16),
-            VMEM((WIDTH, 3 * rows), BF16),
             VMEM((4, rows, WIDTH), F32),
-            VMEM((4, rows, WIDTH), BF16),
-            VMEM((4, rows, WIDTH), BF16),
             VMEM((rows, WIDTH), F32),
             VMEM((GROUP, BLOCKS, BLOCK), F32),
+            VMEM((GROUP, BLOCK, BLOCK), F32),
         ],
-        compiler_params=pltpu.CompilerParams(vmem_limit_bytes=40 << 20),
+        compiler_params=pltpu.CompilerParams(vmem_limit_bytes=16 << 20),
     )(rel_s, head_s, tail_s, count_s, head, t_cols, t_rows, relw, negs, mask)
 
 
 def reduce_kernel(
-    hg, tg, listed, ent, rel,
-    lists, tin, out, fin, tfin, tsend, trecv, ysend, yrecv, p, sz, fz, full, peer,
+    hg, listed, xt, g_hi, g_lo, ent, rel,
+    tg, lists, tin, out, fin, tfin, tsend, trecv, ysend, yrecv, p, sz, fz, full, peer,
     ls, lr, ts, tr, xs, xr, us, ur, vs, vr, ps, pr, rzs, rzr, bys, byr, azs, azr, gxs, gxr, gcs, gcr,
 ):
     x, y, z, core = place()
@@ -406,7 +413,26 @@
     far_dev = device(x, y + 5 * sign, z_there, 1 - core)
     is_head = core == 0
     is_next = core == 1
-    greet(x_peers + x_over + y_peers + z_peers + [other, near_dev, far_dev])
+    partners = x_peers + x_over + y_peers + z_peers + [other, near_dev, far_dev]
+    barrier = pltpu.get_barrier_semaphore()
+    for partner in partners:
+        pl.semaphore_signal(barrier, inc=1, device_id=partner, device_id_type=MESH)
+
+    def tail_products(first):
+        def add_group(g, carry):
+            for n in (first, first + 1):
+                weights = jnp.concatenate([g_hi[g, n], g_hi[g, n], g_lo[g, n]], axis=0)
+                products = jnp.dot(xt[g], weights, preferred_element_type=F32)
+                tg[n, 0] += products[:, 0:BLOCK]
+                tg[n, 1] += products[:, BLOCK:]
+            return carry
+
+        for n in (first, first + 1):
+            tg[n] = jnp.zeros(tg.shape[1:], F32)
+        lax.fori_loop(0, xt.shape[0], add_group, 0)
+
+    tail_products(0)
+    pl.semaphore_wait(barrier, len(partners))
     me = core * 4 + x
     tiles = listed.shape[1] - 8
 
@@ -440,6 +466,13 @@
 
     sent_blocks = (0, 2, 1, 4, 6, 5)
 
+    @pl.when(is_next)
+    def _():
+        for i in sent_blocks:
+            head_x(i, hg.at[head_block(i)]).start()
+
+    tail_products(2)
+
     @pl.when(is_head)
     def _():
         for k in (1, 3, 2):
@@ -448,8 +481,6 @@
     @pl.when(is_next)
     def _():
         to_other.start()
-        for i in sent_blocks:
-            head_x(i, hg.at[head_block(i)]).start()
 
     seven = remote(lists.at[pl.ds(0, 7)], lists.at[pl.ds(0, 7)], ls, lr, other)
     seven.wait_recv()
@@ -625,7 +656,7 @@
         swap(k).wait_send()
 
 
-def reduce(hg, tg, listed, relations):
+def reduce(hg, listed, xt, g_hi, g_lo, relations):
     whole = pl.BlockSpec(memory_space=VMEM)
     dma = pltpu.SemaphoreType.DMA
     rows = listed.shape[1]
@@ -633,9 +664,10 @@
         reduce_kernel,
         name="reduce_gradients",
         out_shape=(jax.ShapeDtypeStruct((BLOCK, WIDTH), F32), jax.ShapeDtypeStruct((relations, WIDTH), F32)),
-        in_specs=[whole] * 3,
+        in_specs=[whole] * 5,
         out_specs=(whole, whole),
         scratch_shapes=[
+            VMEM((4, 2, WIDTH, BLOCK), F32),
             VMEM((8, rows, 128), F32),
             VMEM((4, 2, WIDTH, BLOCK), F32),
             VMEM((BLOCKS, BLOCK, WIDTH), F32),
@@ -661,14 +693,14 @@
             dma((3,)), dma((3,)),
             dma((4,)), dma((4,)),
         ],
-        compiler_params=pltpu.CompilerParams(collective_id=1, has_side_effects=True, vmem_limit_bytes=40 << 20),
-    )(hg, tg, listed)
+        compiler_params=pltpu.CompilerParams(collective_id=1, has_side_effects=True, vmem_limit_bytes=24 << 20),
+    )(hg, listed, xt, g_hi, g_lo)
 
 
 def local(entity, rel_weight, tile_rel, tile_head, tile_tail, tile_mask, negatives, tile_count):
     ready = gather(entity, rel_weight, negatives, tile_mask, tile_rel, tile_head, tile_tail)
-    hg, tg, listed = terms(*ready, tile_count)
-    return reduce(hg, tg, listed, rel_weight.shape[0])
+    hg, listed, xt, g_hi, g_lo = terms(*ready, tile_count)
+    return reduce(hg, listed, xt, g_hi, g_lo, rel_weight.shape[0])
 
 
 def solution(mesh):

time: 104 us -> 106 us (1.019)
  Pallas kernels: 101 us -> 103 us
    pallas_call x1, Pallas kernels: 50.5 us -> 57.2 us  [reduce(): pl.pallas_call(reduce_kernel, name='reduce_gradients', out_shape=(jax.Sha...]
    pallas_call x1, Pallas kernels: 13.4 us -> 9.24 us  [terms(): pl.pallas_call(terms_kernel, name='tile_terms', out_shape=(part, jax.Shap...]
where the time goes in v4:
time: 106 us
  Pallas kernels  103 us (97%)
  local copies, waits for them, and re-layouts  1.58 us (1%)
  between operations  1.3 us (1%)
    pallas_call x1, Pallas kernels, reduce(): pl.pallas_call(reduce_kernel, name='reduce_gradients', out_shape=(jax.Sha...  57.2 us
    pallas_call x1, Pallas kernels, gather(): pl.pallas_call(gather_kernel, name='gather_partitions', out_shape=(part,...  37 us
    pallas_call x1, Pallas kernels, terms(): pl.pallas_call(terms_kernel, name='tile_terms', out_shape=(part, jax.Shap...  9.24 us

profile of v4, /device:TPU:1, one launch (start us, length us, event | category | flops | bytes accessed | tf_op | source)
XLA Modules:
  0.0 106.3 jit_solution(3233994515357265474)
XLA Ops:
  1.3 37.0 %gather_partitions.1 = (f32[8,128,256]{2,1,0:T(8,128)S(1)}, bf16[1024,768]{1,0:T(8,128)(2,1)S(1)}, bf16[4,768,256]{2,1,0:T(8,128)(2,1)S(1)}, f32[900,256]{1,0:T(...) custom-call(f32[128,256]{1,0:T(8,128)} %own_ref.1, ...), custom_call_target="tpu_custom_call" | custom-call | tf_op jit(solution)/shard_map/gather_partitions/pallas_call | solution.py:243
  38.3 9.2 %tile_terms.1 = (f32[8,128,256]{2,1,0:T(8,128)S(1)}, f32[2,40,128]{2,1,0:T(8,128)S(1)}, bf16[4,256,3072]{2,1,0:T(8,128)(2,1)S(1)}, bf16[4,4,1024,256]{3,2,1,0:T(8,128)(2,1)S(1)}, bf16[4,4,1024,256]{3,2,1,0:T(8,128)(2,1)S(1)}) custom-call(s32[32]{0:T(128)S(1)} %get-tuple-element.16.rel_s, s32[32]{0:T(128)S(1)} %get-tuple-element.17.head_s, ...), custom_call_target="tpu_custom_call" | custom-call | tf_op jit(solution)/shard_map/tile_terms/pallas_call | solution.py:373
  47.5 57.2 %reduce_gradients.1 = (f32[128,256]{1,0:T(8,128)S(1)}, f32[900,256]{1,0:T(8,128)S(1)}) custom-call(f32[8,128,256]{2,1,0:T(8,128)S(1)} %get-tuple-element.25.hg, f32[2,40,128]{2,1,0:T(8,128)S(1)} %get-tuple-element.26.listed, bf16[4,256,3072]{2,1,0:T(8,128)(2,1)S(1)} %get-tuple-element.27.xt, bf16[4,4,1024,256]{3,2,1,0:T(8,128)(2,1)S(1)} %get-tuple-element.28.g_hi, ...), custom_call_target="tpu_custom_call" | custom-call | tf_op jit(solution)/shard_map/reduce_gradients/pallas_call | solution.py:663
  104.7 0.7 copy.13
  105.4 0.9 copy.14

commit v5 on v3

--- a/solution.py
+++ b/solution.py
@@ -265,7 +265,7 @@
 
 def terms_kernel(
     rel_s, head_s, tail_s, count_s, head, t_cols, t_rows, relw, negs, mask, hgrad, tgrad, listed,
-    xx, xt, scores, g_hi, g_lo, mixed, counts,
+    xx, xt, scores, g_hi, g_lo, mixed, counts, edges,
 ):
     count = count_s[0]
     parts = 4
@@ -306,24 +306,26 @@
         def make_scores(n):
             scores[n] = dot_nt(xx[...], t_cols[pl.ds(n * step, step), :])
 
+        def make_edges(j):
+            tile = group * GROUP + j
+            b = tail_s[tile]
+            at = pl.ds(pl.multiple_of((b % 2) * BLOCK, BLOCK), BLOCK)
+            own = scores[b // 2, pl.ds(j * BLOCK, BLOCK), at]
+            live = jnp.where(tile < count, 1.0, 0.0).astype(F32)
+            edges[j] = (mask[tile].astype(F32) * live) * lax.logistic(-own)
+
         def make_grads(n):
             for j in range(GROUP):
                 tile = group * GROUP + j
-                alive = tile < count
                 at = pl.ds(j * BLOCK, BLOCK)
-                marked = mask[tile].astype(F32)
                 for h in range(2):
                     b = 2 * n + h
-                    s = scores[n, at, h * BLOCK:(h + 1) * BLOCK]
-                    e = jnp.exp(-jnp.abs(s))
-                    big = 1.0 / (1.0 + e)
-                    small = e * big
-                    up = s >= 0.0
-                    here = jnp.where(jnp.logical_and(alive, tail_s[tile] == b), 1.0, 0.0).astype(F32)
-                    g = counts[j, b:b + 1, :] * jnp.where(up, big, small) - (marked * here) * jnp.where(up, small, big)
+                    lanes = slice(h * BLOCK, (h + 1) * BLOCK)
+                    here = jnp.where(tail_s[tile] == b, 1.0, 0.0).astype(F32)
+                    g = counts[j, b:b + 1, :] * lax.logistic(scores[n, at, lanes]) - here * edges[j]
                     hi, lo = halves(g)
-                    g_hi[n, at, h * BLOCK:(h + 1) * BLOCK] = hi
-                    g_lo[n, at, h * BLOCK:(h + 1) * BLOCK] = lo
+                    g_hi[n, at, lanes] = hi
+                    g_lo[n, at, lanes] = lo
 
         def make_tail(n):
             weights = jnp.concatenate([g_hi[n], g_hi[n], g_lo[n]], axis=0)
@@ -339,10 +341,11 @@
             else:
                 mixed[...] += part
 
-        make_scores(0)
         for n in range(parts):
-            if n + 1 < parts:
-                make_scores(n + 1)
+            make_scores(n)
+        for j in range(GROUP):
+            make_edges(j)
+        for n in range(parts):
             make_grads(n)
             make_mixed(n)
             make_tail(n)
@@ -381,6 +384,7 @@
             VMEM((4, rows, WIDTH), BF16),
             VMEM((rows, WIDTH), F32),
             VMEM((GROUP, BLOCKS, BLOCK), F32),
+            VMEM((GROUP, BLOCK, BLOCK), F32),
         ],
         compiler_params=pltpu.CompilerParams(vmem_limit_bytes=40 << 20),
     )(rel_s, head_s, tail_s, count_s, head, t_cols, t_rows, relw, negs, mask)

time: 104 us -> 101 us (0.971)
  Pallas kernels: 101 us -> 98.7 us
    pallas_call x1, Pallas kernels: 13.4 us -> 6.71 us  [terms(): pl.pallas_call(terms_kernel, name='tile_terms', out_shape=(part, jax.Shap...]
    pallas_call x1, Pallas kernels: 50.5 us -> 55 us  [reduce(): pl.pallas_call(reduce_kernel, name='reduce_gradients', out_shape=(jax.Sha...]
where the time goes in v5:
time: 101 us; the launch traced here: 102 us
  Pallas kernels  98.7 us (98%)
  local copies, waits for them, and re-layouts  1.58 us (2%)
  between operations  1.3 us (1%)
    pallas_call x1, Pallas kernels, reduce(): pl.pallas_call(reduce_kernel, name='reduce_gradients', out_shape=(jax.Sha...  55 us
    pallas_call x1, Pallas kernels, gather(): pl.pallas_call(gather_kernel, name='gather_partitions', out_shape=(part,...  37 us
    pallas_call x1, Pallas kernels, terms(): pl.pallas_call(terms_kernel, name='tile_terms', out_shape=(part, jax.Shap...  6.71 us

profile of v5, /device:TPU:1, one launch (start us, length us, event | category | flops | bytes accessed | tf_op | source)
XLA Modules:
  0.0 101.6 jit_solution(5825403285410998286)
XLA Ops:
  1.3 37.0 %gather_partitions.1 = (f32[8,128,256]{2,1,0:T(8,128)S(1)}, bf16[1024,768]{1,0:T(8,128)(2,1)S(1)}, bf16[4,768,256]{2,1,0:T(8,128)(2,1)S(1)}, f32[900,256]{1,0:T(...) custom-call(f32[128,256]{1,0:T(8,128)} %own_ref.1, ...), custom_call_target="tpu_custom_call" | custom-call | tf_op jit(solution)/shard_map/gather_partitions/pallas_call | solution.py:243
  38.3 6.7 %tile_terms.1 = (f32[8,128,256]{2,1,0:T(8,128)S(1)}, f32[4,2,256,128]{3,2,1,0:T(8,128)S(1)}, f32[2,40,128]{2,1,0:T(8,128)S(1)}) custom-call(s32[32]{0:T(128)S(1)} %get-tuple-element.14.rel_s, s32[32]{0:T(128)S(1)} %get-tuple-element.15.head_s, s32[32]{0:T(128)S(1)} %get-tuple-element.16.tail_s, s32[1]{0:T(128)S(6)} %copy.12.count_s, ...), custom_call_target="tpu_custom_call" | custom-call | tf_op jit(solution)/shard_map/tile_terms/pallas_call | solution.py:373
  45.0 55.0 %reduce_gradients.1 = (f32[128,256]{1,0:T(8,128)S(1)}, f32[900,256]{1,0:T(8,128)S(1)}) custom-call(f32[8,128,256]{2,1,0:T(8,128)S(1)} %get-tuple-element.23.hg, f32[4,2,256,128]{3,2,1,0:T(8,128)S(1)} %get-tuple-element.24.tg, f32[2,40,128]{2,1,0:T(8,128)S(1)} %get-tuple-element.25.listed), custom_call_target="tpu_custom_call" | custom-call | tf_op jit(solution)/shard_map/reduce_gradients/pallas_call | solution.py:636
  100.0 0.7 copy.13
  100.7 0.9 copy.14

commit v6 on v5

--- a/solution.py
+++ b/solution.py
@@ -515,15 +515,6 @@
     for k in range(1, 8):
         remote(fz.at[0], fz.at[k], bys, byr, y_peers[k - 1]).start()
 
-    @pl.when(is_head)
-    def _():
-        for k in range(1, 4):
-            tail_x(k).wait_recv()
-        for c, parity in ((0, q_down), (1, 1 - q_down)):
-            tsend[c] = tg[x, parity] + tfin[0, parity] + tfin[1, parity] + tfin[2, parity]
-        tail_y(0, near_dev).start()
-        tail_y(1, far_dev).start()
-
 
     all_of(fz.at[pl.ds(1, 7)], bys, byr).wait_recv()
     acc = fz[(y + 8) % 8]
@@ -542,6 +533,15 @@
 
     for k in range(1, 8):
         third_z(k).start()
+
+    @pl.when(is_head)
+    def _():
+        for k in range(1, 4):
+            tail_x(k).wait_recv()
+        for c, parity in ((0, q_down), (1, 1 - q_down)):
+            tsend[c] = tg[x, parity] + tfin[0, parity] + tfin[1, parity] + tfin[2, parity]
+        tail_y(0, near_dev).start()
+        tail_y(1, far_dev).start()
 
     ysend[...] = x_total(0)
     along_y = remote(ysend, yrecv, ps, pr, pair)

time: 101 us -> 102 us (level); the launches traced: 102 us -> 101 us
  no operation moved by 1% of the time
where the time goes in v6:
time: 102 us; the launch traced here: 101 us
  Pallas kernels  98.2 us (96%)
  local copies, waits for them, and re-layouts  1.58 us (2%)
  between operations  1.3 us (1%)
    pallas_call x1, Pallas kernels, reduce(): pl.pallas_call(reduce_kernel, name='reduce_gradients', out_shape=(jax.Sha...  54.5 us
    pallas_call x1, Pallas kernels, gather(): pl.pallas_call(gather_kernel, name='gather_partitions', out_shape=(part,...  37 us
    pallas_call x1, Pallas kernels, terms(): pl.pallas_call(terms_kernel, name='tile_terms', out_shape=(part, jax.Shap...  6.71 us

profile of v6, /device:TPU:1, one launch (start us, length us, event | category | flops | bytes accessed | tf_op | source)
XLA Modules:
  0.0 101.0 jit_solution(17052962256180098868)
XLA Ops:
  1.3 37.0 %gather_partitions.1 = (f32[8,128,256]{2,1,0:T(8,128)S(1)}, bf16[1024,768]{1,0:T(8,128)(2,1)S(1)}, bf16[4,768,256]{2,1,0:T(8,128)(2,1)S(1)}, f32[900,256]{1,0:T(...) custom-call(f32[128,256]{1,0:T(8,128)} %own_ref.1, ...), custom_call_target="tpu_custom_call" | custom-call | tf_op jit(solution)/shard_map/gather_partitions/pallas_call | solution.py:243
  38.3 6.7 %tile_terms.1 = (f32[8,128,256]{2,1,0:T(8,128)S(1)}, f32[4,2,256,128]{3,2,1,0:T(8,128)S(1)}, f32[2,40,128]{2,1,0:T(8,128)S(1)}) custom-call(s32[32]{0:T(128)S(1)} %get-tuple-element.14.rel_s, s32[32]{0:T(128)S(1)} %get-tuple-element.15.head_s, s32[32]{0:T(128)S(1)} %get-tuple-element.16.tail_s, s32[1]{0:T(128)S(6)} %copy.12.count_s, ...), custom_call_target="tpu_custom_call" | custom-call | tf_op jit(solution)/shard_map/tile_terms/pallas_call | solution.py:373
  45.0 54.5 %reduce_gradients.1 = (f32[128,256]{1,0:T(8,128)S(1)}, f32[900,256]{1,0:T(8,128)S(1)}) custom-call(f32[8,128,256]{2,1,0:T(8,128)S(1)} %get-tuple-element.23.hg, f32[4,2,256,128]{3,2,1,0:T(8,128)S(1)} %get-tuple-element.24.tg, f32[2,40,128]{2,1,0:T(8,128)S(1)} %get-tuple-element.25.listed), custom_call_target="tpu_custom_call" | custom-call | tf_op jit(solution)/shard_map/reduce_gradients/pallas_call | solution.py:636
  99.5 0.7 copy.13
  100.1 0.9 copy.14
